TPU v7x, 512 devices: a whole 4x8x8 slice. The times are simulated.
512 devices in a mesh: ctx: 32 (over z, y_hi), exp: 8 (over x, y_lo), rep: 2 (over core).
Axes of the slice: x: 4, y: 8 (y_hi: 4, y_lo: 2; y = y_hi * 2 + y_lo), z: 8, core: 2. Of those that a mesh axis runs over, the one named last changes fastest.
Arguments:
- queries: bfloat16 [4096, 4096], P(('rep', 'ctx'), 'exp'), parts along dimension 0, may hold values from -8 to 8
- key_rows: bfloat16 [4096, 256], P(('rep', 'ctx')), parts along dimension 0, may hold values from -8 to 8
- value_head_rows: bfloat16 [4096, 256], P(('rep', 'ctx')), parts along dimension 0, may hold values from -6 to 6
- block_order: int32 [64], P('rep'), parts along dimension 0, may hold values from 0 to 31, each once
- residual: bfloat16 [4096, 4096], P(('rep', 'ctx'), 'exp'), parts along dimension 0, may hold values from -8 to 8
- norm_gain: float32 [4096], P('exp'), may hold values from 0.25 to 1.75
- expert_ids: int32 [4096, 8], P(('rep', 'ctx')), parts along dimension 0, may hold values from 0 to 63, all different within a row; in each aligned block of 64 rows (0 to 63, 64 to 127, ...) at most 16 rows name the same one
- route_weight: float32 [4096, 8], P(('rep', 'ctx')), parts along dimension 0, may hold values from 0.02 to 0.5
- gate_weight: bfloat16 [64, 4096, 768], P('ctx', 'exp'), may hold values from -0.09375 to 0.09375
- up_weight: bfloat16 [64, 4096, 768], P('ctx', 'exp'), may hold values from -0.09375 to 0.09375
- down_weight: bfloat16 [64, 768, 4096], P('ctx', None, 'exp'), may hold values from -0.21875 to 0.21875
Outputs:
- layer_out: bfloat16 [4096, 4096], P(('rep', 'ctx'), 'exp'), parts along dimension 0
There are 2 independent parts, one for each index of `rep`. A program takes and returns all parts, laid end to end along the dimension named above; an argument that names none is the same for every part. Nothing has to cross between parts.
Inputs may be any that keep to these rules, and one draw needn't show every extreme that they name: `expert_ids`: each row names 8 different experts. In each aligned block of 64 rows no expert is named by more than 16 rows, a bound that some block reaches. `block_order`: each block index appears once.
All inputs are finite; a program needn't handle non-finite values.
Results may differ from a plain program's by a relative error of at most 0.011.
Values may be sent and summed in bfloat16 or wider, within the bound.
A program may use at most 64 MiB of HBM per device.

v0:
```python
import math

import jax
import jax.numpy as jnp
from jax import lax
from jax.sharding import PartitionSpec as P

D = 4096
QUERY_HEADS = 32
KEY_VALUE_HEADS = 2
HEAD_SIZE = 128
TOPK = 8
EXP_ROW = 2


MASKED_SCORE = -1e30
NORM_EPS = 1e-06


def local(
    queries,
    key_rows,
    value_head_rows,
    block_order,
    residual,
    norm_gain,
    expert_ids,
    route_weight,
    gate_weight,
    up_weight,
    down_weight,
):
    shard_rows = queries.shape[0]
    ctx_count = lax.axis_size("ctx")
    local_head = queries.shape[1] // HEAD_SIZE
    expert_index = lax.axis_index("exp")
    ctx_index = lax.axis_index("ctx")
    key_value_head = expert_index * local_head // (QUERY_HEADS // KEY_VALUE_HEADS)
    my_keys = lax.dynamic_slice_in_dim(key_rows, key_value_head * HEAD_SIZE, HEAD_SIZE, 1)
    my_values = lax.dynamic_slice_in_dim(value_head_rows, key_value_head * HEAD_SIZE, HEAD_SIZE, 1)
    block_ids = jnp.arange(ctx_count, dtype=jnp.int32)
    own_block = jnp.sum(jnp.where(block_ids == ctx_index, block_order, 0))
    local_rows = jnp.arange(shard_rows, dtype=jnp.int32)
    query_pos = jnp.tile(own_block * shard_rows + local_rows, local_head)
    query_flat = (
        queries.reshape(shard_rows, local_head, HEAD_SIZE)
        .transpose(1, 0, 2)
        .reshape(local_head * shard_rows, HEAD_SIZE)
    )
    inv_scale = 1.0 / math.sqrt(HEAD_SIZE)
    query_count = local_head * shard_rows
    running_max = jnp.full((query_count,), MASKED_SCORE, jnp.float32)
    piece_keys = lax.all_gather(my_keys, "ctx", axis=0, tiled=True)
    piece_values = lax.all_gather(my_values, "ctx", axis=0, tiled=True)
    key_index = jnp.arange(piece_keys.shape[0], dtype=jnp.int32)
    owner_shard = key_index // shard_rows
    key_block = jnp.sum(
        jnp.where(owner_shard[:, None] == block_ids[None, :], block_order[None, :], 0), axis=1
    )
    key_pos = key_block * shard_rows + key_index % shard_rows
    visible = key_pos[None, :] <= query_pos[:, None]
    scores = (
        lax.dot_general(
            query_flat, piece_keys, (((1,), (1,)), ((), ())), preferred_element_type=jnp.float32
        )
        * inv_scale
    )
    scores = jnp.where(visible, scores, MASKED_SCORE)
    newest = jnp.maximum(running_max, jnp.max(scores, axis=1))
    weights = jnp.where(visible, jnp.exp(scores - newest[:, None]), 0.0)
    running_sum = jnp.sum(weights, axis=1)
    weighted = jnp.dot(
        weights.astype(jnp.bfloat16), piece_values, preferred_element_type=jnp.float32
    )
    running_max, running_sum, weighted = (newest, running_sum, weighted)
    attention = (
        (weighted / running_sum[:, None])
        .reshape(local_head, shard_rows, HEAD_SIZE)
        .transpose(1, 0, 2)
        .reshape(shard_rows, local_head * HEAD_SIZE)
        .astype(jnp.bfloat16)
    )
    mixed_rows = (residual.astype(jnp.float32) + attention.astype(jnp.float32)).astype(jnp.bfloat16)
    mixed_f = mixed_rows.astype(jnp.float32)
    square_sum = lax.psum(jnp.sum(mixed_f * mixed_f, axis=1), "exp")
    normed = (mixed_f * lax.rsqrt(square_sum[:, None] / D + NORM_EPS) * norm_gain[None, :]).astype(
        jnp.bfloat16
    )
    expert_count = ctx_count * EXP_ROW
    capacity = 2 * shard_rows * TOPK // expert_count
    flat_ids = expert_ids.reshape(-1)
    onehot = (flat_ids[:, None] == jnp.arange(expert_count, dtype=jnp.int32)[None, :]).astype(
        jnp.int32
    )
    slot_rank = jnp.sum((jnp.cumsum(onehot, axis=0) - onehot) * onehot, axis=1)
    slot_index = flat_ids * capacity + slot_rank
    source_rows = jnp.arange(shard_rows * TOPK, dtype=jnp.int32) // TOPK
    outgoing = (
        jnp.zeros((expert_count * capacity, normed.shape[1]), jnp.bfloat16)
        .at[slot_index]
        .set(normed[source_rows])
    )
    outgoing = outgoing.reshape(ctx_count, EXP_ROW, capacity, normed.shape[1])
    incoming = lax.all_to_all(outgoing, "ctx", split_axis=0, concat_axis=0, tiled=True)
    gate_part = jnp.einsum(
        "skcd,kdh->skch", incoming, gate_weight, preferred_element_type=jnp.float32
    ).astype(jnp.bfloat16)
    up_part = jnp.einsum(
        "skcd,kdh->skch", incoming, up_weight, preferred_element_type=jnp.float32
    ).astype(jnp.bfloat16)
    gate_full, up_full = (
        lax.psum(gate_part, "exp").astype(jnp.float32),
        lax.psum(up_part, "exp").astype(jnp.float32),
    )
    hidden = (jax.nn.silu(gate_full) * up_full).astype(jnp.bfloat16)
    expert_out = jnp.einsum(
        "skch,khd->skcd", hidden, down_weight, preferred_element_type=jnp.float32
    ).astype(jnp.bfloat16)
    returned = lax.all_to_all(expert_out, "ctx", split_axis=0, concat_axis=0, tiled=True)
    flat_back = returned.reshape(expert_count * capacity, normed.shape[1])
    picked = flat_back[slot_index].astype(jnp.float32).reshape(shard_rows, TOPK, normed.shape[1])
    routed_sum = jnp.sum(route_weight[:, :, None] * picked, axis=1)
    return (mixed_f + routed_sum).astype(jnp.bfloat16)


def solution(mesh):
    placed = (
        P(("rep", "ctx"), "exp"),
        P(("rep", "ctx"), None),
        P(("rep", "ctx"), None),
        P("rep"),
        P(("rep", "ctx"), "exp"),
        P("exp"),
        P(("rep", "ctx"), None),
        P(("rep", "ctx"), None),
        P("ctx", "exp", None),
        P("ctx", "exp", None),
        P("ctx", None, "exp"),
    )
    return jax.shard_map(
        local, mesh=mesh, in_specs=placed, out_specs=P(("rep", "ctx"), "exp"), check_vma=False
    )
```

profile of v0, /device:TPU:11, one launch (start us, length us, event | category | flops | bytes accessed | tf_op | source)
XLA Modules:
  0.0 449.2 jit_solution(4844218175703528937)
XLA Ops:
  6.5 0.0 copy-start
  6.5 0.0 copy-start.2
  6.5 0.0 all-reduce.3.cloned.1.call-start
  6.5 0.9 copy.45
  7.4 0.1 eq.55
  7.5 0.1 eq.51
  7.6 0.7 broadcast_multiply_fusion
  8.3 0.7 constant_dynamic-slice_fusion.1
  9.1 76.4 %all_gather.6 = bf16[2048,128]{1,0:T(8,128)(2,1)S(1)} all-gather(bf16[64,128]{1,0:T(8,128)(2,1)S(1)} %constant_dynamic-slice_fusion.1), channel_id=1, replica_groups=mesh['ctx'=32,'exp'=8,'rep'=2] {'ctx'}, dimensions={0}, use_global_device_ids=true | all-gather | bytes 540672 | tf_op jit(solution)/shard_map/all_gather | solution.py:53
  85.5 1.3 fusion.58
  87.4 0.1 le.16
  87.5 0.8 select_reduce_fusion
  88.3 0.9 reshape.155
  89.2 0.5 fusion.62
  89.7 0.0 copy-done.2
  89.8 64.6 %all_gather.7 = bf16[2048,128]{1,0:T(8,128)(2,1)S(1)} all-gather(bf16[64,128]{1,0:T(8,128)(2,1)S(1)} %constant_dynamic-slice_fusion), channel_id=1, replica_groups=mesh['ctx'=32,'exp'=8,'rep'=2] {'ctx'}, dimensions={0}, use_global_device_ids=true | all-gather | bytes 540672 | tf_op jit(solution)/shard_map/all_gather | solution.py:54
  154.4 0.5 fusion.7
  154.9 0.0 copy-start.1
  154.9 0.0 copy-start.4
  154.9 0.8 fusion.30
  155.7 0.0 copy-done.1
  155.7 0.1 fusion.41
  155.8 12.2 %psum.21 = f32[64]{0:T(128)S(1)} all-reduce(f32[64]{0:T(128)S(1)} %get-tuple-element.7), channel_id=1, replica_groups=mesh['ctx'=32,'exp'=8,'rep'=2] {'exp'}, use_global_device_ids=true, to_apply=%region_8.9 | all-reduce | flops 64 | bytes 512 | tf_op jit(solution)/shard_map/psum | solution.py:85
  168.0 1.2 reduce-window.6
  169.2 0.2 slice_reduce_fusion
  169.5 0.1 copy.44
  169.6 0.1 mul.90
  169.7 0.1 fusion.47
  169.8 0.0 copy-done.4
  169.8 0.1 fusion.43
  169.9 5.0 %scatter_custom_fusion = bf16[1024,512]{1,0:T(8,128)(2,1)S(1)} fusion(s32[512]{0:T(512)S(1)} %bitcast.82, bf16[64,512]{1,0:T(8,128)(2,1)S(1)} %fusion.43, s32[1024]{0:T(1024)S(1)} %pad_clamp_fusion.1, bf16[]{:T(256)} %constant.99.clone.1), kind=kCustom, calls=%fused_computation.35 | custom fusion | bytes 1048578 | tf_op jit(solution)/shard_map/scatter | solution.py:101
  175.0 22.3 %all_to_all.10 = bf16[32,2,16,512]{3,2,1,0:T(8,128)(2,1)S(1)} all-to-all(bf16[32,2,16,512]{3,2,1,0:T(8,128)(2,1)S(1)} %bitcast.77), channel_id=1, replica_groups=mesh['ctx'=32,'exp'=8,'rep'=2] {'ctx'}, dimensions={0} | all-to-all | bytes 2097152 | tf_op jit(solution)/shard_map/all_to_all | solution.py:104
  197.3 0.0 copy-done
  197.3 0.0 copy-start.5
  197.3 2.2 fusion.19
  199.5 0.0 copy-done.5
  199.5 2.1 fusion.22
  201.6 0.0 copy-start.6
  201.6 0.0 all-reduce.3.cloned.1.call-update
  201.7 186.1 %all-reduce.3.cloned.1.call-done = (bf16[32,2,16,768]{3,2,0,1:T(8,128)(2,1)}, bf16[32,2,16,768]{3,2,0,1:T(8,128)(2,1)}) async-done(((bf16[32,2,16,768]{3,2,0,1:T(8,128)(2,1)}, bf16[32,2,16,768]{3,2,0,1:T(8,128)(2,1)}), (bf16[32,2,16,768]{3,2,0,1:T(8,128)(2,1)}, bf16[32,2,16,768]{3,2,0,1:T(8,128)(2,1)})) %all-reduce.3.cloned.1.call-update) | async-done | bytes 3145744 | tf_op jit(solution)/shard_map/psum | solution.py:113
  387.8 0.0 copy-done.6
  387.8 3.0 fusion.25
  390.8 0.0 copy-start.3
  390.8 1.1 copy.50
  391.9 12.4 %all-to-all-start.1 = ((bf16[32,2,16,512]{3,2,1,0:T(8,128)(2,1)}), bf16[32,2,16,512]{3,2,1,0:T(8,128)(2,1)S(1)}, u32[]{:S(2)}, u32[]{:S(2)}) async-start(bf16[32,2,16,512]{3,2,1,0:T(8,128)(2,1)} %copy.50), calls=%async_computation.1 | async-start | bytes 2097152 | tf_op jit(solution)/shard_map/all_to_all | solution.py:119
  404.3 0.0 copy-done.3
  404.3 0.1 copy.43
  404.4 35.0 %all-to-all-done.1 = bf16[32,2,16,512]{3,2,1,0:T(8,128)(2,1)S(1)} async-done(((bf16[32,2,16,512]{3,2,1,0:T(8,128)(2,1)}), bf16[32,2,16,512]{3,2,1,0:T(8,128)(2,1)S(1)}, u32[]{:S(2)}, u32[]{:S(2)}) %all-to-all-start.1) | async-done | bytes 1048608 | tf_op jit(solution)/shard_map/all_to_all | solution.py:119
  439.4 2.0 gather_fusion
  441.4 0.4 fusion.31
  441.8 0.6 fusion.44
  (15 shorter events, 0.1 us)
Async XLA Ops:
  6.5 190.8 %copy-start = (bf16[2,512,768]{2,1,0:T(8,128)(2,1)S(1)}, bf16[2,512,768]{2,1,0:T(8,128)(2,1)}, u32[]{:S(2)}) copy-start(bf16[2,512,768]{2,1,0:T(8,128)(2,1)} %param.19) | copy-start | bytes 4718596
  6.5 83.2 %copy-start.2 = (bf16[64,256]{1,0:T(8,128)(2,1)S(1)}, bf16[64,256]{1,0:T(8,128)(2,1)}, u32[]{:S(2)}) copy-start(bf16[64,256]{1,0:T(8,128)(2,1)} %param.13) | copy-start | bytes 98308
  6.5 381.3 %all-reduce.3.cloned.1.call-start = ((), (), s32[]{:S(2)}) async-start(), calls=%async_computation.2 | async-start | bytes 6291456 | tf_op jit(solution)/shard_map/psum | solution.py:113
  154.9 0.9 copy-start.1
  154.9 15.0 %copy-start.4 = (f32[512]{0:T(512)S(1)}, f32[512]{0:T(512)}, u32[]{:S(2)}) copy-start(f32[512]{0:T(512)} %param.16) | copy-start | bytes 6148
  197.3 2.2 copy-start.5
  201.6 186.2 %copy-start.6 = (bf16[2,768,512]{2,1,0:T(8,128)(2,1)S(1)}, bf16[2,768,512]{2,1,0:T(8,128)(2,1)}, u32[]{:S(2)}) copy-start(bf16[2,768,512]{2,1,0:T(8,128)(2,1)} %param.21) | copy-start | bytes 4718596
  390.8 13.5 %copy-start.3 = (f32[64,8]{0,1:T(8,128)S(1)}, f32[64,8]{0,1:T(8,128)}, u32[]{:S(2)}) copy-start(f32[64,8]{0,1:T(8,128)} %param.18) | copy-start | bytes 6148
  391.9 47.5 %all-to-all-start.1 = ((bf16[32,2,16,512]{3,2,1,0:T(8,128)(2,1)}), bf16[32,2,16,512]{3,2,1,0:T(8,128)(2,1)S(1)}, u32[]{:S(2)}, u32[]{:S(2)}) async-start(bf16[32,2,16,512]{3,2,1,0:T(8,128)(2,1)} %copy.50), calls=%async_computation.1 | async-start | bytes 2097152 | tf_op jit(solution)/shard_map/all_to_all | solution.py:119
Sparse Core Ops, SparseCore 0:
  201.8 185.9 all-reduce.2
where the time goes:
time: 450 us; the launch traced here: 449 us
  waiting for transfers between devices  221 us (49%)
  blocking collectives  175 us (39%)
  between operations  14.3 us (3%)
  starting transfers between devices  12.4 us (3%)
  local copies, waits for them, and re-layouts  11.4 us (3%)
  matrix products  8.63 us (2%)
  other arithmetic  5.88 us (1%)
    psum x1, waiting for transfers between devices, local(): lax.psum(up_part, 'exp').astype(jnp.float32)  186 us
    all_gather x1, blocking collectives, local(): piece_keys = lax.all_gather(my_keys, 'ctx', axis=0, tiled=True)  76.4 us
    all_gather x1, blocking collectives, local(): piece_values = lax.all_gather(my_values, 'ctx', axis=0, tiled=True)  64.6 us
    all_to_all x1, waiting for transfers between devices, local(): lax.all_to_all(expert_out, 'ctx', split_axis=0, concat_axis=0, tiled=True)  35 us
    all_to_all x1, blocking collectives, local(): lax.all_to_all(outgoing, 'ctx', split_axis=0, concat_axis=0, tiled=True)  22.3 us
    all_to_all x1, starting transfers between devices, local(): lax.all_to_all(expert_out, 'ctx', split_axis=0, concat_axis=0, tiled=True)  12.4 us
    psum x1, blocking collectives, local(): square_sum = lax.psum(jnp.sum(mixed_f * mixed_f, axis=1), 'exp')  12.2 us
  transfers between devices with their start and end apart: 2, of which 2 were waited for; matrix products, arithmetic and copies ran while one was open for 0% of the time, Pallas kernels for 0%

commit v1 on v0

--- a/solution.py
+++ b/solution.py
@@ -1,8 +1,11 @@
+import functools
 import math
 
 import jax
 import jax.numpy as jnp
 from jax import lax
+from jax.experimental import pallas as pl
+from jax.experimental.pallas import tpu as pltpu
 from jax.sharding import PartitionSpec as P
 
 D = 4096
@@ -12,9 +15,59 @@
 TOPK = 8
 EXP_ROW = 2
 
-
 MASKED_SCORE = -1e30
 NORM_EPS = 1e-06
+MESH = pl.DeviceIdType.MESH
+
+
+def exchange_kernel(axis, n, gather, n_in, *refs):
+    ins, outs = refs[:n_in], refs[n_in : 2 * n_in]
+    send_sem, recv_sem = refs[2 * n_in], refs[2 * n_in + 1]
+    me = lax.axis_index(axis)
+    barrier = pltpu.get_barrier_semaphore()
+    for k in range(1, n):
+        pl.semaphore_signal(
+            barrier, inc=1, device_id={axis: lax.rem(me + k, n)}, device_id_type=MESH
+        )
+    pl.semaphore_wait(barrier, n - 1)
+    copies = []
+    for k in range(1, n):
+        peer = lax.rem(me + k, n)
+        for i in range(n_in):
+            copy = pltpu.make_async_remote_copy(
+                src_ref=ins[i] if gather else ins[i].at[peer],
+                dst_ref=outs[i].at[me],
+                send_sem=send_sem.at[i, k],
+                recv_sem=recv_sem.at[i, k],
+                device_id={axis: peer},
+                device_id_type=MESH,
+            )
+            copy.start()
+            copies.append(copy)
+    for i in range(n_in):
+        outs[i][me] = ins[i][...] if gather else ins[i][me]
+    for copy in copies:
+        copy.wait()
+
+
+def exchange(xs, axis, n, gather, collective_id):
+    n_in = len(xs)
+    out_shape = [
+        jax.ShapeDtypeStruct((n,) + (x.shape if gather else x.shape[1:]), x.dtype) for x in xs
+    ]
+    nbytes = sum(x.size * x.dtype.itemsize for x in xs) * (n if gather else 1)
+    return pl.pallas_call(
+        functools.partial(exchange_kernel, axis, n, gather, n_in),
+        out_shape=out_shape,
+        in_specs=[pl.BlockSpec(memory_space=pltpu.VMEM)] * n_in,
+        out_specs=[pl.BlockSpec(memory_space=pltpu.VMEM)] * n_in,
+        scratch_shapes=[
+            pltpu.SemaphoreType.DMA((n_in, n)),
+            pltpu.SemaphoreType.DMA((n_in, n)),
+        ],
+        compiler_params=pltpu.CompilerParams(collective_id=collective_id, has_side_effects=True),
+        cost_estimate=pl.CostEstimate(flops=0, bytes_accessed=2 * nbytes, transcendentals=0),
+    )(*xs)
 
 
 def local(
@@ -32,6 +85,7 @@
 ):
     shard_rows = queries.shape[0]
     ctx_count = lax.axis_size("ctx")
+    exp_count = lax.axis_size("exp")
     local_head = queries.shape[1] // HEAD_SIZE
     expert_index = lax.axis_index("exp")
     ctx_index = lax.axis_index("ctx")
@@ -48,10 +102,12 @@
         .reshape(local_head * shard_rows, HEAD_SIZE)
     )
     inv_scale = 1.0 / math.sqrt(HEAD_SIZE)
-    query_count = local_head * shard_rows
-    running_max = jnp.full((query_count,), MASKED_SCORE, jnp.float32)
-    piece_keys = lax.all_gather(my_keys, "ctx", axis=0, tiled=True)
-    piece_values = lax.all_gather(my_values, "ctx", axis=0, tiled=True)
+    (key_value_all,) = exchange(
+        [jnp.concatenate([my_keys, my_values], axis=1)], "ctx", ctx_count, True, 0
+    )
+    key_value_all = key_value_all.reshape(ctx_count * shard_rows, 2 * HEAD_SIZE)
+    piece_keys = key_value_all[:, :HEAD_SIZE]
+    piece_values = key_value_all[:, HEAD_SIZE:]
     key_index = jnp.arange(piece_keys.shape[0], dtype=jnp.int32)
     owner_shard = key_index // shard_rows
     key_block = jnp.sum(
@@ -66,13 +122,12 @@
         * inv_scale
     )
     scores = jnp.where(visible, scores, MASKED_SCORE)
-    newest = jnp.maximum(running_max, jnp.max(scores, axis=1))
+    newest = jnp.max(scores, axis=1)
     weights = jnp.where(visible, jnp.exp(scores - newest[:, None]), 0.0)
     running_sum = jnp.sum(weights, axis=1)
     weighted = jnp.dot(
         weights.astype(jnp.bfloat16), piece_values, preferred_element_type=jnp.float32
     )
-    running_max, running_sum, weighted = (newest, running_sum, weighted)
     attention = (
         (weighted / running_sum[:, None])
         .reshape(local_head, shard_rows, HEAD_SIZE)
@@ -82,7 +137,10 @@
     )
     mixed_rows = (residual.astype(jnp.float32) + attention.astype(jnp.float32)).astype(jnp.bfloat16)
     mixed_f = mixed_rows.astype(jnp.float32)
-    square_sum = lax.psum(jnp.sum(mixed_f * mixed_f, axis=1), "exp")
+    square_part = jnp.sum(mixed_f * mixed_f, axis=1)
+    square_block = jnp.pad(square_part.reshape(1, shard_rows), ((0, 7), (0, 128 - shard_rows)))
+    (square_all,) = exchange([square_block], "exp", exp_count, True, 1)
+    square_sum = jnp.sum(square_all, axis=0)[0, :shard_rows]
     normed = (mixed_f * lax.rsqrt(square_sum[:, None] / D + NORM_EPS) * norm_gain[None, :]).astype(
         jnp.bfloat16
     )
@@ -101,22 +159,32 @@
         .set(normed[source_rows])
     )
     outgoing = outgoing.reshape(ctx_count, EXP_ROW, capacity, normed.shape[1])
-    incoming = lax.all_to_all(outgoing, "ctx", split_axis=0, concat_axis=0, tiled=True)
+    (incoming,) = exchange([outgoing], "ctx", ctx_count, False, 2)
     gate_part = jnp.einsum(
         "skcd,kdh->skch", incoming, gate_weight, preferred_element_type=jnp.float32
     ).astype(jnp.bfloat16)
     up_part = jnp.einsum(
         "skcd,kdh->skch", incoming, up_weight, preferred_element_type=jnp.float32
     ).astype(jnp.bfloat16)
-    gate_full, up_full = (
-        lax.psum(gate_part, "exp").astype(jnp.float32),
-        lax.psum(up_part, "exp").astype(jnp.float32),
-    )
-    hidden = (jax.nn.silu(gate_full) * up_full).astype(jnp.bfloat16)
+    slot_count = ctx_count * EXP_ROW * capacity
+    hid = gate_part.shape[-1]
+    chunk = slot_count // exp_count
+    gate_recv, up_recv = exchange(
+        [gate_part.reshape(exp_count, chunk, hid), up_part.reshape(exp_count, chunk, hid)],
+        "exp",
+        exp_count,
+        False,
+        3,
+    )
+    gate_full = jnp.sum(gate_recv.astype(jnp.float32), axis=0)
+    up_full = jnp.sum(up_recv.astype(jnp.float32), axis=0)
+    hidden_mine = (jax.nn.silu(gate_full) * up_full).astype(jnp.bfloat16)
+    (hidden,) = exchange([hidden_mine], "exp", exp_count, True, 4)
+    hidden = hidden.reshape(ctx_count, EXP_ROW, capacity, hid)
     expert_out = jnp.einsum(
         "skch,khd->skcd", hidden, down_weight, preferred_element_type=jnp.float32
     ).astype(jnp.bfloat16)
-    returned = lax.all_to_all(expert_out, "ctx", split_axis=0, concat_axis=0, tiled=True)
+    (returned,) = exchange([expert_out], "ctx", ctx_count, False, 5)
     flat_back = returned.reshape(expert_count * capacity, normed.shape[1])
     picked = flat_back[slot_index].astype(jnp.float32).reshape(shard_rows, TOPK, normed.shape[1])
     routed_sum = jnp.sum(route_weight[:, :, None] * picked, axis=1)

time: 450 us -> 262 us (0.58)
  the two profiles are of different devices: /device:TPU:11 before, /device:TPU:96 now
where the time goes in v1:
time: 262 us; the launch traced here: 261 us
  Pallas kernels  226 us (86%)
  local copies, waits for them, and re-layouts  16.1 us (6%)
  other arithmetic  9.38 us (4%)
  matrix products  9.14 us (3%)
    pallas_call x6, Pallas kernels, exchange(): pl.pallas_call(functools.partial(exchange_kernel, axis, n, gather, n_in),...  226 us
    scatter x1, local copies, waits for them, and re-layouts, local(): outgoing = jnp.zeros((expert_count * capacity, normed.shape[1]), jnp.bflo...  5.8 us

profile of v1, /device:TPU:96, one launch (start us, length us, event | category | flops | bytes accessed | tf_op | source)
XLA Modules:
  0.0 261.4 jit_solution(6058986128674041762)
XLA Ops:
  0.0 0.0 copy-start
  0.0 0.9 constant_dynamic-slice_fusion
  0.9 0.6 pad_maximum_fusion.refs_0_
  1.5 42.8 %shard_map.109 = bf16[32,64,256]{2,1,0:T(8,128)(2,1)} custom-call(bf16[64,256]{1,0:T(8,128)(2,1)} %pad_maximum_fusion.refs_0_), custom_call_target="tpu_custom_call" | custom-call | bytes 2097152 | tf_op jit(solution)/shard_map/pallas_call | solution.py:59
  44.3 1.3 fusion.50
  46.3 0.1 le.16
  46.4 0.8 select_reduce_fusion
  47.1 0.9 reshape.181
  48.0 0.0 copy-start.2
  48.0 1.8 fusion.53
  49.8 0.5 fusion.2
  50.3 0.0 copy-done.2
  50.3 0.0 copy-start.4
  50.3 0.0 copy-start.7
  50.3 0.0 copy-start.5
  50.4 0.8 fusion.20
  51.2 0.0 copy-done.4
  51.2 0.1 fusion.33
  51.3 0.6 pad.4.refs_0_
  51.9 8.9 %shard_map.110 = f32[8,8,128]{2,1,0:T(8,128)} custom-call(f32[8,128]{1,0:T(8,128)} %pad.4.refs_0_), custom_call_target="tpu_custom_call" | custom-call | bytes 65536 | tf_op jit(solution)/shard_map/pallas_call | solution.py:59
  60.8 0.8 reduce_sum.89
  61.6 0.0 copy-done.7
  61.6 0.1 fusion.35
  61.7 0.0 copy-done.5
  61.7 0.1 copy.49
  61.8 0.1 eq.55
  61.9 1.2 reduce-window.6
  63.1 0.2 slice_reduce_fusion
  63.4 0.1 eq.51
  63.4 0.1 fusion.39
  63.6 0.1 copy.48
  63.7 0.1 mul.90
  63.8 5.8 %scatter_custom_fusion = bf16[1024,512]{1,0:T(8,128)(2,1)} fusion(s32[512]{0:T(512)S(1)} %bitcast.91, bf16[64,512]{1,0:T(8,128)(2,1)S(1)} %fusion.35, s32[1024]{0:T(1024)S(1)} %pad_clamp_fusion.1, bf16[]{:T(256)} %constant.99.clone.1), kind=kCustom, calls=%fused_computation.32 | custom fusion | bytes 1048578 | tf_op jit(solution)/shard_map/scatter | solution.py:159
  69.6 44.8 %shard_map.111 = bf16[32,2,16,512]{3,2,1,0:T(8,128)(2,1)} custom-call(bf16[32,2,16,512]{3,2,1,0:T(8,128)(2,1)} %bitcast.83), custom_call_target="tpu_custom_call" | custom-call | bytes 2097152 | tf_op jit(solution)/shard_map/pallas_call | solution.py:59
  114.4 0.0 copy-done
  114.5 2.2 fusion.11
  116.7 0.0 copy-start.3
  116.7 0.0 copy-start.8
  116.7 1.4 copy.53
  118.1 0.0 copy-done.3
  118.1 0.9 copy-done.8
  119.0 1.0 fusion.14
  120.0 1.4 copy.55
  121.3 38.2 %shard_map.112 = (bf16[8,128,768]{2,1,0:T(8,128)(2,1)}, bf16[8,128,768]{2,1,0:T(8,128)(2,1)}) custom-call(bf16[8,128,768]{2,1,0:T(8,128)(2,1)} %bitcast.81, bf16[8,128,768]{2,1,0:T(8,128)(2,1)} %bitcast.82), custom_call_target="tpu_custom_call" | custom-call | bytes 6291456 | tf_op jit(solution)/shard_map/pallas_call | solution.py:59
  159.6 0.0 copy-start.1
  159.6 1.8 convert_reduce_fusion
  161.4 0.1 copy-done.1
  161.5 0.0 copy-start.9
  161.5 0.2 convert_reduce_fusion.1
  161.7 0.8 multiply_convert_fusion.refs_0_
  162.5 22.9 %shard_map.113 = bf16[8,128,768]{2,1,0:T(8,128)(2,1)} custom-call(bf16[128,768]{1,0:T(8,128)(2,1)} %multiply_convert_fusion.refs_0_), custom_call_target="tpu_custom_call" | custom-call | bytes 3145728 | tf_op jit(solution)/shard_map/pallas_call | solution.py:59
  185.4 0.0 copy-done.9
  185.4 3.4 %fusion.17.refs_0_ = bf16[32,2,16,512]{3,2,1,0:T(8,128)(2,1)} fusion(bf16[32,2,16,768]{3,2,1,0:T(8,128)(2,1)} %bitcast.84, bf16[2,768,512]{2,1,0:T(8,128)(2,1)S(1)} %copy-done.9), kind=kOutput, calls=%fused_computation.20 | convolution fusion | flops 805830656 | bytes 4194304 | tf_op jit(solution)/shard_map/skch,khd->skcd/dot_general | solution.py:184
  188.7 68.1 %shard_map.114 = bf16[32,2,16,512]{3,2,1,0:T(8,128)(2,1)} custom-call(bf16[32,2,16,512]{3,2,1,0:T(8,128)(2,1)} %fusion.17.refs_0_), custom_call_target="tpu_custom_call" | custom-call | bytes 2097152 | tf_op jit(solution)/shard_map/pallas_call | solution.py:59
  256.9 0.0 copy-start.6
  256.9 3.3 %gather_fusion = bf16[512,512]{1,0:T(8,128)(2,1)S(1)} fusion(bf16[1024,512]{1,0:T(8,128)(2,1)} %bitcast.80, s32[1024]{0:T(1024)S(1)} %pad_clamp_fusion), kind=kCustom, calls=%fused_computation.1 | custom fusion | bytes 1050624 | tf_op jit(solution)/shard_map/gather | solution.py:189
  260.3 0.0 copy-done.6
  260.3 0.1 copy.47
  260.4 0.4 fusion.21
  260.7 0.6 fusion.36
  (14 shorter events, 0.1 us)
Async XLA Ops:
  0.0 114.5 %copy-start = (bf16[2,512,768]{2,1,0:T(8,128)(2,1)S(1)}, bf16[2,512,768]{2,1,0:T(8,128)(2,1)}, u32[]{:S(2)}) copy-start(bf16[2,512,768]{2,1,0:T(8,128)(2,1)} %param.19) | copy-start | bytes 4718596
  48.0 2.3 copy-start.2
  50.3 0.9 copy-start.4
  50.3 11.2 %copy-start.7 = (f32[512]{0:T(512)S(1)}, f32[512]{0:T(512)}, u32[]{:S(2)}) copy-start(f32[512]{0:T(512)} %param.16) | copy-start | bytes 6148
  50.3 11.3 %copy-start.5 = (s32[64,8]{0,1:T(8,128)S(1)}, s32[64,8]{0,1:T(8,128)}, u32[]{:S(2)}) copy-start(s32[64,8]{0,1:T(8,128)} %param.17) | copy-start | bytes 6148
  116.7 1.4 copy-start.3
  116.7 2.3 copy-start.8
  159.6 1.9 copy-start.1
  161.5 23.9 %copy-start.9 = (bf16[2,768,512]{2,1,0:T(8,128)(2,1)S(1)}, bf16[2,768,512]{2,1,0:T(8,128)(2,1)}, u32[]{:S(2)}) copy-start(bf16[2,768,512]{2,1,0:T(8,128)(2,1)} %param.21) | copy-start | bytes 4718596
  256.9 3.4 %copy-start.6 = (f32[64,8]{0,1:T(8,128)S(1)}, f32[64,8]{0,1:T(8,128)}, u32[]{:S(2)}) copy-start(f32[64,8]{0,1:T(8,128)} %param.18) | copy-start | bytes 6148

commit v2 on v1

--- a/solution.py
+++ b/solution.py
@@ -68,6 +68,126 @@
         compiler_params=pltpu.CompilerParams(collective_id=collective_id, has_side_effects=True),
         cost_estimate=pl.CostEstimate(flops=0, bytes_accessed=2 * nbytes, transcendentals=0),
     )(*xs)
+
+
+def dispatch_reduce_kernel(n_ctx, n_exp, *refs):
+    (outgoing, gate_w, up_w, gate_recv, up_recv, incoming, gate_stage, up_stage,
+     d_send, d_recv, r_send, r_recv) = refs
+    per_chunk = n_ctx // n_exp
+    me_c = lax.axis_index("ctx")
+    me_e = lax.axis_index("exp")
+    plane = me_c // per_chunk
+    barrier = pltpu.get_barrier_semaphore()
+    for k in range(1, n_ctx):
+        pl.semaphore_signal(
+            barrier, inc=1, device_id={"ctx": lax.rem(me_c + k, n_ctx)}, device_id_type=MESH
+        )
+    for k in range(1, n_exp):
+        pl.semaphore_signal(
+            barrier, inc=1, device_id={"exp": lax.rem(me_e + k, n_exp)}, device_id_type=MESH
+        )
+    pl.semaphore_wait(barrier, n_ctx + n_exp - 2)
+
+    def dispatch_copy(p):
+        return pltpu.make_async_remote_copy(
+            src_ref=outgoing.at[p],
+            dst_ref=incoming.at[me_c],
+            send_sem=d_send.at[p],
+            recv_sem=d_recv.at[me_c],
+            device_id={"ctx": p},
+            device_id_type=MESH,
+        )
+
+    for t in range(n_exp):
+        z_r = lax.rem(plane + 2 * n_exp - me_e - t, n_exp)
+        for y in range(per_chunk):
+            p = z_r * per_chunk + y
+
+            @pl.when(p != me_c)
+            def _():
+                dispatch_copy(p).start()
+
+            @pl.when(p == me_c)
+            def _():
+                pltpu.make_async_copy(outgoing.at[p], incoming.at[p], d_recv.at[p]).start()
+
+    parts = ((gate_w, gate_stage, gate_recv), (up_w, up_stage, up_recv))
+
+    def reduce_copy(j, which):
+        _, stage, recv = parts[which]
+        return pltpu.make_async_remote_copy(
+            src_ref=stage.at[j],
+            dst_ref=recv.at[me_e],
+            send_sem=r_send.at[j, which],
+            recv_sem=r_recv.at[me_e, which],
+            device_id={"exp": j},
+            device_id_type=MESH,
+        )
+
+    rows = gate_stage.shape[2]
+    for t in range(n_exp):
+        j = lax.rem(plane + me_e + t, n_exp)
+        for y in range(per_chunk):
+            s = j * per_chunk + y
+            pltpu.make_async_copy(incoming.at[s], incoming.at[s], d_recv.at[s]).wait()
+        first = pl.multiple_of(j * per_chunk, per_chunk)
+        for k in range(EXP_ROW):
+            x = incoming[pl.ds(first, per_chunk), k].reshape(rows, incoming.shape[-1])
+            for w, stage, _ in parts:
+                stage[j, k] = jnp.dot(x, w[k], preferred_element_type=jnp.float32).astype(
+                    stage.dtype
+                )
+
+        @pl.when(j != me_e)
+        def _():
+            for which in range(2):
+                reduce_copy(j, which).start()
+
+        @pl.when(j == me_e)
+        def _():
+            for which, (_, stage, recv) in enumerate(parts):
+                pltpu.make_async_copy(stage.at[j], recv.at[j], r_recv.at[j, which]).start()
+
+    for s in range(n_exp):
+        for which, (_, _, recv) in enumerate(parts):
+            pltpu.make_async_copy(recv.at[s], recv.at[s], r_recv.at[s, which]).wait()
+    for j in range(n_exp):
+
+        @pl.when(j != me_e)
+        def _():
+            for which in range(2):
+                reduce_copy(j, which).wait_send()
+
+    for p in range(n_ctx):
+
+        @pl.when(p != me_c)
+        def _():
+            dispatch_copy(p).wait_send()
+
+
+def dispatch_reduce(outgoing, gate_weight, up_weight, n_ctx, n_exp, collective_id):
+    hid = gate_weight.shape[-1]
+    slots = outgoing.shape[0] * outgoing.shape[2] // n_exp
+    recv_shape = jax.ShapeDtypeStruct((n_exp, EXP_ROW, slots, hid), jnp.bfloat16)
+    flops = 2 * 2 * outgoing.size * hid
+    nbytes = 2 * outgoing.size * 2 + 4 * gate_weight.size * 2 + 4 * n_exp * EXP_ROW * slots * hid * 2
+    return pl.pallas_call(
+        functools.partial(dispatch_reduce_kernel, n_ctx, n_exp),
+        out_shape=[recv_shape, recv_shape],
+        in_specs=[pl.BlockSpec(memory_space=pltpu.VMEM)] * 3,
+        out_specs=[pl.BlockSpec(memory_space=pltpu.VMEM)] * 2,
+        scratch_shapes=[
+            pltpu.VMEM(outgoing.shape, outgoing.dtype),
+            pltpu.VMEM(recv_shape.shape, jnp.bfloat16),
+            pltpu.VMEM(recv_shape.shape, jnp.bfloat16),
+            pltpu.SemaphoreType.DMA((n_ctx,)),
+            pltpu.SemaphoreType.DMA((n_ctx,)),
+            pltpu.SemaphoreType.DMA((n_exp, 2)),
+            pltpu.SemaphoreType.DMA((n_exp, 2)),
+        ],
+        compiler_params=pltpu.CompilerParams(collective_id=collective_id, has_side_effects=True),
+        cost_estimate=pl.CostEstimate(flops=flops, bytes_accessed=nbytes, transcendentals=0),
+    )(outgoing, gate_weight, up_weight)
 
 
 def local(
@@ -159,31 +279,20 @@
         .set(normed[source_rows])
     )
     outgoing = outgoing.reshape(ctx_count, EXP_ROW, capacity, normed.shape[1])
-    (incoming,) = exchange([outgoing], "ctx", ctx_count, False, 2)
-    gate_part = jnp.einsum(
-        "skcd,kdh->skch", incoming, gate_weight, preferred_element_type=jnp.float32
-    ).astype(jnp.bfloat16)
-    up_part = jnp.einsum(
-        "skcd,kdh->skch", incoming, up_weight, preferred_element_type=jnp.float32
-    ).astype(jnp.bfloat16)
-    slot_count = ctx_count * EXP_ROW * capacity
-    hid = gate_part.shape[-1]
-    chunk = slot_count // exp_count
-    gate_recv, up_recv = exchange(
-        [gate_part.reshape(exp_count, chunk, hid), up_part.reshape(exp_count, chunk, hid)],
-        "exp",
-        exp_count,
-        False,
-        3,
-    )
+    gate_recv, up_recv = dispatch_reduce(outgoing, gate_weight, up_weight, ctx_count, exp_count, 2)
     gate_full = jnp.sum(gate_recv.astype(jnp.float32), axis=0)
     up_full = jnp.sum(up_recv.astype(jnp.float32), axis=0)
     hidden_mine = (jax.nn.silu(gate_full) * up_full).astype(jnp.bfloat16)
     (hidden,) = exchange([hidden_mine], "exp", exp_count, True, 4)
-    hidden = hidden.reshape(ctx_count, EXP_ROW, capacity, hid)
     expert_out = jnp.einsum(
-        "skch,khd->skcd", hidden, down_weight, preferred_element_type=jnp.float32
+        "jksh,khd->jksd", hidden, down_weight, preferred_element_type=jnp.float32
     ).astype(jnp.bfloat16)
+    per_chunk = ctx_count // exp_count
+    expert_out = (
+        expert_out.reshape(exp_count, EXP_ROW, per_chunk, capacity, normed.shape[1])
+        .transpose(0, 2, 1, 3, 4)
+        .reshape(ctx_count, EXP_ROW, capacity, normed.shape[1])
+    )
     (returned,) = exchange([expert_out], "ctx", ctx_count, False, 5)
     flat_back = returned.reshape(expert_count * capacity, normed.shape[1])
     picked = flat_back[slot_index].astype(jnp.float32).reshape(shard_rows, TOPK, normed.shape[1])

time: 262 us -> 256 us (0.977)
  the two profiles are of different devices: /device:TPU:96 before, /device:TPU:1 now
where the time goes in v2:
time: 256 us
  Pallas kernels  227 us (89%)
  local copies, waits for them, and re-layouts  13.6 us (5%)
  other arithmetic  9.51 us (4%)
  matrix products  4.98 us (2%)
    pallas_call x4, Pallas kernels, exchange(): pl.pallas_call(functools.partial(exchange_kernel, axis, n, gather, n_in),...  142 us
    pallas_call x1, Pallas kernels, dispatch_reduce(): pl.pallas_call(functools.partial(dispatch_reduce_kernel, n_ctx, n_exp), o...  84.1 us
    scatter x1, local copies, waits for them, and re-layouts, local(): outgoing = jnp.zeros((expert_count * capacity, normed.shape[1]), jnp.bflo...  5.79 us

profile of v2, /device:TPU:1, one launch (start us, length us, event | category | flops | bytes accessed | tf_op | source)
XLA Modules:
  0.0 255.6 jit_solution(1246764755081077206)
XLA Ops:
  0.0 0.0 copy-start
  0.0 0.9 constant_dynamic-slice_fusion
  0.9 0.6 pad_maximum_fusion.1.refs_0_
  1.5 49.5 %shard_map.109 = bf16[32,64,256]{2,1,0:T(8,128)(2,1)} custom-call(bf16[64,256]{1,0:T(8,128)(2,1)} %pad_maximum_fusion.1.refs_0_), custom_call_target="tpu_custom_call" | custom-call | bytes 2097152 | tf_op jit(solution)/shard_map/pallas_call | solution.py:59
  50.9 1.3 fusion.45
  52.9 0.1 le.16
  53.0 0.8 select_reduce_fusion
  53.8 0.9 reshape.176
  54.7 0.0 copy-start.2
  54.7 1.8 fusion.49
  56.4 0.5 fusion.2
  57.0 0.0 copy-done.2
  57.0 0.0 copy-start.3
  57.0 0.0 copy-start.6
  57.0 0.0 copy-start.4
  57.0 0.8 fusion.17
  57.8 0.0 copy-done.3
  57.8 0.1 fusion.28
  58.0 0.6 pad.4.refs_0_
  58.6 7.7 %shard_map.110 = f32[8,8,128]{2,1,0:T(8,128)} custom-call(f32[8,128]{1,0:T(8,128)} %pad.4.refs_0_), custom_call_target="tpu_custom_call" | custom-call | bytes 65536 | tf_op jit(solution)/shard_map/pallas_call | solution.py:59
  66.3 0.8 reduce_sum.89
  67.1 0.0 copy-done.6
  67.1 0.1 fusion.30
  67.2 0.0 copy-done.4
  67.2 0.1 copy.37
  67.3 0.1 eq.55
  67.4 1.2 reduce-window.6
  68.6 0.2 slice_reduce_fusion
  68.9 0.1 eq.51
  68.9 0.1 fusion.34
  69.1 0.1 copy.36
  69.2 0.1 mul.90
  69.3 5.8 %scatter_custom_fusion = bf16[1024,512]{1,0:T(8,128)(2,1)} fusion(s32[512]{0:T(512)S(1)} %bitcast.70, bf16[64,512]{1,0:T(8,128)(2,1)S(1)} %fusion.30, s32[1024]{0:T(1024)S(1)} %pad_clamp_fusion.1, bf16[]{:T(256)} %constant.99.clone.1), kind=kCustom, calls=%fused_computation.26 | custom fusion | bytes 1048578 | tf_op jit(solution)/shard_map/scatter | solution.py:279
  75.1 84.1 %shard_map.111 = (bf16[8,2,64,768]{3,2,1,0:T(8,128)(2,1)}, bf16[8,2,64,768]{3,2,1,0:T(8,128)(2,1)}) custom-call(bf16[32,2,16,512]{3,2,1,0:T(8,128)(2,1)} %bitcast.65, bf16[2,512,768]{2,1,0:T(8,128)(2,1)} %refs_1_.1, bf16[2,512,768]{2,1,0:T(8,128)(2,1)} %refs_2_.1), custom_call_target="tpu_custom_call" | custom-call | flops 1610612736 | bytes 14680064 | tf_op jit(solution)/shard_map/pallas_call | solution.py:174
  159.2 0.0 copy-start.1
  159.2 1.8 convert_reduce_fusion
  160.9 0.1 copy-done.1
  161.0 0.2 convert_reduce_fusion.1
  161.3 0.8 multiply_convert_fusion.refs_0_
  162.0 24.7 %shard_map.112 = bf16[8,2,64,768]{3,2,1,0:T(8,128)(2,1)} custom-call(bf16[2,64,768]{2,1,0:T(8,128)(2,1)} %multiply_convert_fusion.refs_0_), custom_call_target="tpu_custom_call" | custom-call | bytes 3145728 | tf_op jit(solution)/shard_map/pallas_call | solution.py:59
  186.8 0.0 copy-done
  186.8 2.4 fusion.12
  189.2 0.1 fusion.48
  189.3 0.1 pad_maximum_fusion
  189.4 1.1 copy.41
  190.5 60.6 %shard_map.113 = bf16[32,2,16,512]{3,2,1,0:T(8,128)(2,1)} custom-call(bf16[32,2,16,512]{3,2,1,0:T(8,128)(2,1)} %bitcast.62), custom_call_target="tpu_custom_call" | custom-call | bytes 2097152 | tf_op jit(solution)/shard_map/pallas_call | solution.py:59
  251.1 0.0 copy-start.5
  251.1 3.3 %gather_fusion = bf16[512,512]{1,0:T(8,128)(2,1)S(1)} fusion(bf16[1024,512]{1,0:T(8,128)(2,1)} %bitcast.61, s32[1024]{0:T(1024)S(1)} %pad_clamp_fusion), kind=kCustom, calls=%fused_computation.1 | custom fusion | bytes 1050624 | tf_op jit(solution)/shard_map/gather | solution.py:298
  254.5 0.0 copy-done.5
  254.5 0.1 copy.35
  254.6 0.4 fusion.18
  254.9 0.6 fusion.31
  (14 shorter events, 0.1 us)
Async XLA Ops:
  0.0 186.8 %copy-start = (bf16[2,768,512]{2,1,0:T(8,128)(2,1)S(1)}, bf16[2,768,512]{2,1,0:T(8,128)(2,1)}, u32[]{:S(2)}) copy-start(bf16[2,768,512]{2,1,0:T(8,128)(2,1)} %param.21) | copy-start | bytes 4718596
  54.7 2.3 copy-start.2
  57.0 0.9 copy-start.3
  57.0 10.1 %copy-start.6 = (f32[512]{0:T(512)S(1)}, f32[512]{0:T(512)}, u32[]{:S(2)}) copy-start(f32[512]{0:T(512)} %param.16) | copy-start | bytes 6148
  57.0 10.2 %copy-start.4 = (s32[64,8]{0,1:T(8,128)S(1)}, s32[64,8]{0,1:T(8,128)}, u32[]{:S(2)}) copy-start(s32[64,8]{0,1:T(8,128)} %param.17) | copy-start | bytes 6148
  159.2 1.9 copy-start.1
  251.1 3.4 %copy-start.5 = (f32[64,8]{0,1:T(8,128)S(1)}, f32[64,8]{0,1:T(8,128)}, u32[]{:S(2)}) copy-start(f32[64,8]{0,1:T(8,128)} %param.18) | copy-start | bytes 6148

commit v3 on v2

--- a/solution.py
+++ b/solution.py
@@ -188,6 +188,102 @@
         compiler_params=pltpu.CompilerParams(collective_id=collective_id, has_side_effects=True),
         cost_estimate=pl.CostEstimate(flops=flops, bytes_accessed=nbytes, transcendentals=0),
     )(outgoing, gate_weight, up_weight)
+
+
+def kv_gather_kernel(n_ctx, n_exp, group, *refs):
+    block, kv_all, s1_send, s1_recv, s2_send, s2_recv = refs
+    per_plane = n_ctx // n_exp
+    planes = n_ctx // per_plane
+    me_c = lax.axis_index("ctx")
+    me_e = lax.axis_index("exp")
+    q = lax.rem(me_e, group)
+    head_base = me_e - q
+    plane = me_c // per_plane
+    barrier = pltpu.get_barrier_semaphore()
+    for k in range(1, n_ctx):
+        pl.semaphore_signal(
+            barrier, inc=1, device_id={"ctx": lax.rem(me_c + k, n_ctx)}, device_id_type=MESH
+        )
+    for k in range(1, group):
+        pl.semaphore_signal(
+            barrier, inc=1, device_id={"exp": head_base + lax.rem(q + k, group)}, device_id_type=MESH
+        )
+    pl.semaphore_wait(barrier, n_ctx + group - 2)
+
+    def first_copy(p):
+        return pltpu.make_async_remote_copy(
+            src_ref=block,
+            dst_ref=kv_all.at[me_c],
+            send_sem=s1_send.at[p],
+            recv_sem=s1_recv.at[me_c],
+            device_id={"ctx": p},
+            device_id_type=MESH,
+        )
+
+    halves = 2
+    for h in range(halves):
+        z_r = lax.rem(plane + 2 * planes - q - h * (planes // halves), planes)
+        for y in range(per_plane):
+            p = z_r * per_plane + y
+
+            @pl.when(p != me_c)
+            def _():
+                first_copy(p).start()
+
+            @pl.when(p == me_c)
+            def _():
+                pltpu.make_async_copy(block, kv_all.at[p], s1_recv.at[p]).start()
+
+    def second_copy(h, r):
+        first = pl.multiple_of(lax.rem(plane + q + h * (planes // halves), planes) * per_plane, per_plane)
+        return pltpu.make_async_remote_copy(
+            src_ref=kv_all.at[pl.ds(first, per_plane)],
+            dst_ref=kv_all.at[pl.ds(first, per_plane)],
+            send_sem=s2_send.at[r, h],
+            recv_sem=s2_recv.at[r, h],
+            device_id={"exp": head_base + lax.rem(q + r, group)},
+            device_id_type=MESH,
+        )
+
+    for h in range(halves):
+        z_s = lax.rem(plane + q + h * (planes // halves), planes)
+        for y in range(per_plane):
+            s = z_s * per_plane + y
+            pltpu.make_async_copy(kv_all.at[s], kv_all.at[s], s1_recv.at[s]).wait()
+        for r in range(1, group):
+            second_copy(h, r).start()
+    for h in range(halves):
+        for r in range(1, group):
+            second_copy(h, r).wait_recv()
+    for h in range(halves):
+        for r in range(1, group):
+            second_copy(h, r).wait_send()
+    for h in range(halves):
+        z_r = lax.rem(plane + 2 * planes - q - h * (planes // halves), planes)
+        for y in range(per_plane):
+            p = z_r * per_plane + y
+
+            @pl.when(p != me_c)
+            def _():
+                first_copy(p).wait_send()
+
+
+def kv_gather(block, n_ctx, n_exp, group, collective_id):
+    nbytes = block.size * block.dtype.itemsize * n_ctx
+    return pl.pallas_call(
+        functools.partial(kv_gather_kernel, n_ctx, n_exp, group),
+        out_shape=jax.ShapeDtypeStruct((n_ctx,) + block.shape, block.dtype),
+        in_specs=[pl.BlockSpec(memory_space=pltpu.VMEM)],
+        out_specs=pl.BlockSpec(memory_space=pltpu.VMEM),
+        scratch_shapes=[
+            pltpu.SemaphoreType.DMA((n_ctx,)),
+            pltpu.SemaphoreType.DMA((n_ctx,)),
+            pltpu.SemaphoreType.DMA((group, 2)),
+            pltpu.SemaphoreType.DMA((group, 2)),
+        ],
+        compiler_params=pltpu.CompilerParams(collective_id=collective_id, has_side_effects=True),
+        cost_estimate=pl.CostEstimate(flops=0, bytes_accessed=2 * nbytes, transcendentals=0),
+    )(block)
 
 
 def local(
@@ -222,8 +318,12 @@
         .reshape(local_head * shard_rows, HEAD_SIZE)
     )
     inv_scale = 1.0 / math.sqrt(HEAD_SIZE)
-    (key_value_all,) = exchange(
-        [jnp.concatenate([my_keys, my_values], axis=1)], "ctx", ctx_count, True, 0
+    key_value_all = kv_gather(
+        jnp.concatenate([my_keys, my_values], axis=1),
+        ctx_count,
+        exp_count,
+        QUERY_HEADS // KEY_VALUE_HEADS // local_head,
+        0,
     )
     key_value_all = key_value_all.reshape(ctx_count * shard_rows, 2 * HEAD_SIZE)
     piece_keys = key_value_all[:, :HEAD_SIZE]

time: 256 us -> 255 us (level)
  the two profiles are of different devices: /device:TPU:1 before, /device:TPU:48 now
where the time goes in v3:
time: 255 us; the launch traced here: 254 us
  Pallas kernels  225 us (88%)
  local copies, waits for them, and re-layouts  13.6 us (5%)
  other arithmetic  9.51 us (4%)
  matrix products  4.97 us (2%)
    pallas_call x3, Pallas kernels, exchange(): pl.pallas_call(functools.partial(exchange_kernel, axis, n, gather, n_in),...  105 us
    pallas_call x1, Pallas kernels, dispatch_reduce(): pl.pallas_call(functools.partial(dispatch_reduce_kernel, n_ctx, n_exp), o...  81.9 us
    pallas_call x1, Pallas kernels, kv_gather(): pl.pallas_call(functools.partial(kv_gather_kernel, n_ctx, n_exp, group),...  38.1 us
    scatter x1, local copies, waits for them, and re-layouts, local(): outgoing = jnp.zeros((expert_count * capacity, normed.shape[1]), jnp.bflo...  5.79 us

profile of v3, /device:TPU:48, one launch (start us, length us, event | category | flops | bytes accessed | tf_op | source)
XLA Modules:
  0.0 254.2 jit_solution(2167250911224525472)
XLA Ops:
  0.0 0.0 copy-start
  0.0 0.9 constant_dynamic-slice_fusion
  0.9 0.6 pad_maximum_fusion.1.refs_0_
  1.5 38.1 %shard_map.109 = bf16[32,64,256]{2,1,0:T(8,128)(2,1)} custom-call(bf16[64,256]{1,0:T(8,128)(2,1)} %pad_maximum_fusion.1.refs_0_), custom_call_target="tpu_custom_call" | custom-call | bytes 2097152 | tf_op jit(solution)/shard_map/pallas_call | solution.py:273
  39.6 1.3 fusion.45
  41.6 0.1 le.16
  41.7 0.8 select_reduce_fusion
  42.5 0.9 reshape.176
  43.3 0.0 copy-start.2
  43.4 1.8 fusion.49
  45.1 0.5 fusion.2
  45.6 0.0 copy-done.2
  45.6 0.0 copy-start.3
  45.7 0.0 copy-start.6
  45.7 0.0 copy-start.4
  45.7 0.8 fusion.17
  46.5 0.0 copy-done.3
  46.5 0.1 fusion.28
  46.6 0.6 pad.4.refs_0_
  47.2 10.0 %shard_map.110 = f32[8,8,128]{2,1,0:T(8,128)} custom-call(f32[8,128]{1,0:T(8,128)} %pad.4.refs_0_), custom_call_target="tpu_custom_call" | custom-call | bytes 65536 | tf_op jit(solution)/shard_map/pallas_call | solution.py:59
  57.3 0.8 reduce_sum.89
  58.1 0.0 copy-done.6
  58.1 0.1 fusion.30
  58.2 0.0 copy-done.4
  58.2 0.1 copy.37
  58.3 0.1 eq.55
  58.4 1.2 reduce-window.6
  59.6 0.2 slice_reduce_fusion
  59.9 0.1 eq.51
  59.9 0.1 fusion.34
  60.1 0.1 copy.36
  60.2 0.1 mul.90
  60.3 5.8 %scatter_custom_fusion = bf16[1024,512]{1,0:T(8,128)(2,1)} fusion(s32[512]{0:T(512)S(1)} %bitcast.70, bf16[64,512]{1,0:T(8,128)(2,1)S(1)} %fusion.30, s32[1024]{0:T(1024)S(1)} %pad_clamp_fusion.1, bf16[]{:T(256)} %constant.99.clone.1), kind=kCustom, calls=%fused_computation.26 | custom fusion | bytes 1048578 | tf_op jit(solution)/shard_map/scatter | solution.py:379
  66.1 81.9 %shard_map.111 = (bf16[8,2,64,768]{3,2,1,0:T(8,128)(2,1)}, bf16[8,2,64,768]{3,2,1,0:T(8,128)(2,1)}) custom-call(bf16[32,2,16,512]{3,2,1,0:T(8,128)(2,1)} %bitcast.65, bf16[2,512,768]{2,1,0:T(8,128)(2,1)} %refs_1_.1, bf16[2,512,768]{2,1,0:T(8,128)(2,1)} %refs_2_.1), custom_call_target="tpu_custom_call" | custom-call | flops 1610612736 | bytes 14680064 | tf_op jit(solution)/shard_map/pallas_call | solution.py:174
  148.0 0.0 copy-start.1
  148.0 1.8 convert_reduce_fusion
  149.8 0.1 copy-done.1
  149.9 0.2 convert_reduce_fusion.1
  150.1 0.8 multiply_convert_fusion.refs_0_
  150.9 23.9 %shard_map.112 = bf16[8,2,64,768]{3,2,1,0:T(8,128)(2,1)} custom-call(bf16[2,64,768]{2,1,0:T(8,128)(2,1)} %multiply_convert_fusion.refs_0_), custom_call_target="tpu_custom_call" | custom-call | bytes 3145728 | tf_op jit(solution)/shard_map/pallas_call | solution.py:59
  174.8 0.0 copy-done
  174.8 2.4 fusion.12
  177.2 0.1 fusion.48
  177.3 0.1 pad_maximum_fusion
  177.4 1.1 copy.41
  178.5 71.2 %shard_map.113 = bf16[32,2,16,512]{3,2,1,0:T(8,128)(2,1)} custom-call(bf16[32,2,16,512]{3,2,1,0:T(8,128)(2,1)} %bitcast.62), custom_call_target="tpu_custom_call" | custom-call | bytes 2097152 | tf_op jit(solution)/shard_map/pallas_call | solution.py:59
  249.7 0.0 copy-start.5
  249.7 3.3 %gather_fusion = bf16[512,512]{1,0:T(8,128)(2,1)S(1)} fusion(bf16[1024,512]{1,0:T(8,128)(2,1)} %bitcast.61, s32[1024]{0:T(1024)S(1)} %pad_clamp_fusion), kind=kCustom, calls=%fused_computation.1 | custom fusion | bytes 1050624 | tf_op jit(solution)/shard_map/gather | solution.py:398
  253.1 0.0 copy-done.5
  253.1 0.1 copy.35
  253.2 0.4 fusion.18
  253.6 0.6 fusion.31
  (14 shorter events, 0.1 us)
Async XLA Ops:
  0.0 174.8 %copy-start = (bf16[2,768,512]{2,1,0:T(8,128)(2,1)S(1)}, bf16[2,768,512]{2,1,0:T(8,128)(2,1)}, u32[]{:S(2)}) copy-start(bf16[2,768,512]{2,1,0:T(8,128)(2,1)} %param.21) | copy-start | bytes 4718596
  43.3 2.3 copy-start.2
  45.6 0.9 copy-start.3
  45.7 12.4 %copy-start.6 = (f32[512]{0:T(512)S(1)}, f32[512]{0:T(512)}, u32[]{:S(2)}) copy-start(f32[512]{0:T(512)} %param.16) | copy-start | bytes 6148
  45.7 12.5 %copy-start.4 = (s32[64,8]{0,1:T(8,128)S(1)}, s32[64,8]{0,1:T(8,128)}, u32[]{:S(2)}) copy-start(s32[64,8]{0,1:T(8,128)} %param.17) | copy-start | bytes 6148
  148.0 1.9 copy-start.1
  249.7 3.4 %copy-start.5 = (f32[64,8]{0,1:T(8,128)S(1)}, f32[64,8]{0,1:T(8,128)}, u32[]{:S(2)}) copy-start(f32[64,8]{0,1:T(8,128)} %param.18) | copy-start | bytes 6148

commit v4 on v3

--- a/solution.py
+++ b/solution.py
@@ -284,6 +284,114 @@
         compiler_params=pltpu.CompilerParams(collective_id=collective_id, has_side_effects=True),
         cost_estimate=pl.CostEstimate(flops=0, bytes_accessed=2 * nbytes, transcendentals=0),
     )(block)
+
+
+def gather_return_kernel(n_ctx, n_exp, *refs):
+    hidden_mine, down_w, returned, hidden_all, ret_stage, a_send, a_recv, b_send, b_recv = refs
+    per_chunk = n_ctx // n_exp
+    me_c = lax.axis_index("ctx")
+    me_e = lax.axis_index("exp")
+    plane = me_c // per_chunk
+    barrier = pltpu.get_barrier_semaphore()
+    for k in range(1, n_ctx):
+        pl.semaphore_signal(
+            barrier, inc=1, device_id={"ctx": lax.rem(me_c + k, n_ctx)}, device_id_type=MESH
+        )
+    for k in range(1, n_exp):
+        pl.semaphore_signal(
+            barrier, inc=1, device_id={"exp": lax.rem(me_e + k, n_exp)}, device_id_type=MESH
+        )
+    pl.semaphore_wait(barrier, n_ctx + n_exp - 2)
+
+    def gather_copy(r):
+        return pltpu.make_async_remote_copy(
+            src_ref=hidden_mine,
+            dst_ref=hidden_all.at[me_e],
+            send_sem=a_send.at[r],
+            recv_sem=a_recv.at[me_e],
+            device_id={"exp": r},
+            device_id_type=MESH,
+        )
+
+    for t in range(n_exp):
+        r = lax.rem(me_e + 2 * n_exp - plane - t, n_exp)
+
+        @pl.when(r != me_e)
+        def _():
+            gather_copy(r).start()
+
+        @pl.when(r == me_e)
+        def _():
+            pltpu.make_async_copy(hidden_mine, hidden_all.at[r], a_recv.at[r]).start()
+
+    def return_copy(s):
+        return pltpu.make_async_remote_copy(
+            src_ref=ret_stage.at[s],
+            dst_ref=returned.at[me_c],
+            send_sem=b_send.at[s],
+            recv_sem=b_recv.at[me_c],
+            device_id={"ctx": s},
+            device_id_type=MESH,
+        )
+
+    rows = hidden_all.shape[2]
+    for t in range(n_exp):
+        j = lax.rem(me_e + plane + t, n_exp)
+        pltpu.make_async_copy(hidden_all.at[j], hidden_all.at[j], a_recv.at[j]).wait()
+        first = pl.multiple_of(j * per_chunk, per_chunk)
+        for k in range(EXP_ROW):
+            out = jnp.dot(hidden_all[j, k], down_w[k], preferred_element_type=jnp.float32)
+            ret_stage[pl.ds(first, per_chunk), k] = out.astype(ret_stage.dtype).reshape(
+                per_chunk, rows // per_chunk, out.shape[-1]
+            )
+        for y in range(per_chunk):
+            s = j * per_chunk + y
+
+            @pl.when(s != me_c)
+            def _():
+                return_copy(s).start()
+
+            @pl.when(s == me_c)
+            def _():
+                pltpu.make_async_copy(ret_stage.at[s], returned.at[s], b_recv.at[s]).start()
+
+    for s in range(n_ctx):
+        pltpu.make_async_copy(returned.at[s], returned.at[s], b_recv.at[s]).wait()
+    for r in range(n_exp):
+
+        @pl.when(r != me_e)
+        def _():
+            gather_copy(r).wait_send()
+
+    for s in range(n_ctx):
+
+        @pl.when(s != me_c)
+        def _():
+            return_copy(s).wait_send()
+
+
+def gather_return(hidden_mine, down_weight, n_ctx, n_exp, collective_id):
+    hid, width = down_weight.shape[1:]
+    slots = hidden_mine.shape[1]
+    ret_shape = (n_ctx, EXP_ROW, slots * n_exp // n_ctx, width)
+    flops = 2 * n_exp * hidden_mine.size * width
+    nbytes = 2 * n_exp * hidden_mine.size * 2 + down_weight.size * 2 + 4 * n_ctx * EXP_ROW * slots * width * 2 // n_exp
+    return pl.pallas_call(
+        functools.partial(gather_return_kernel, n_ctx, n_exp),
+        out_shape=jax.ShapeDtypeStruct(ret_shape, jnp.bfloat16),
+        in_specs=[pl.BlockSpec(memory_space=pltpu.VMEM)] * 2,
+        out_specs=pl.BlockSpec(memory_space=pltpu.VMEM),
+        scratch_shapes=[
+            pltpu.VMEM((n_exp,) + hidden_mine.shape, jnp.bfloat16),
+            pltpu.VMEM(ret_shape, jnp.bfloat16),
+            pltpu.SemaphoreType.DMA((n_exp,)),
+            pltpu.SemaphoreType.DMA((n_exp,)),
+            pltpu.SemaphoreType.DMA((n_ctx,)),
+            pltpu.SemaphoreType.DMA((n_ctx,)),
+        ],
+        compiler_params=pltpu.CompilerParams(collective_id=collective_id, has_side_effects=True),
+        cost_estimate=pl.CostEstimate(flops=flops, bytes_accessed=nbytes, transcendentals=0),
+    )(hidden_mine, down_weight)
 
 
 def local(
@@ -383,17 +491,7 @@
     gate_full = jnp.sum(gate_recv.astype(jnp.float32), axis=0)
     up_full = jnp.sum(up_recv.astype(jnp.float32), axis=0)
     hidden_mine = (jax.nn.silu(gate_full) * up_full).astype(jnp.bfloat16)
-    (hidden,) = exchange([hidden_mine], "exp", exp_count, True, 4)
-    expert_out = jnp.einsum(
-        "jksh,khd->jksd", hidden, down_weight, preferred_element_type=jnp.float32
-    ).astype(jnp.bfloat16)
-    per_chunk = ctx_count // exp_count
-    expert_out = (
-        expert_out.reshape(exp_count, EXP_ROW, per_chunk, capacity, normed.shape[1])
-        .transpose(0, 2, 1, 3, 4)
-        .reshape(ctx_count, EXP_ROW, capacity, normed.shape[1])
-    )
-    (returned,) = exchange([expert_out], "ctx", ctx_count, False, 5)
+    returned = gather_return(hidden_mine, down_weight, ctx_count, exp_count, 4)
     flat_back = returned.reshape(expert_count * capacity, normed.shape[1])
     picked = flat_back[slot_index].astype(jnp.float32).reshape(shard_rows, TOPK, normed.shape[1])
     routed_sum = jnp.sum(route_weight[:, :, None] * picked, axis=1)

time: 255 us -> 231 us (0.906)
  the two profiles are of different devices: /device:TPU:48 before, /device:TPU:64 now
where the time goes in v4:
time: 231 us; the launch traced here: 230 us
  Pallas kernels  205 us (89%)
  local copies, waits for them, and re-layouts  12.3 us (5%)
  other arithmetic  9.39 us (4%)
  matrix products  2.58 us (1%)
    pallas_call x1, Pallas kernels, gather_return(): pl.pallas_call(functools.partial(gather_return_kernel, n_ctx, n_exp), out...  82.8 us
    pallas_call x1, Pallas kernels, dispatch_reduce(): pl.pallas_call(functools.partial(dispatch_reduce_kernel, n_ctx, n_exp), o...  69.3 us
    pallas_call x1, Pallas kernels, kv_gather(): pl.pallas_call(functools.partial(kv_gather_kernel, n_ctx, n_exp, group),...  43 us
    pallas_call x1, Pallas kernels, exchange(): pl.pallas_call(functools.partial(exchange_kernel, axis, n, gather, n_in),...  9.88 us
    scatter x1, local copies, waits for them, and re-layouts, local(): outgoing = jnp.zeros((expert_count * capacity, normed.shape[1]), jnp.bflo...  5.79 us

profile of v4, /device:TPU:64, one launch (start us, length us, event | category | flops | bytes accessed | tf_op | source)
XLA Modules:
  0.0 230.3 jit_solution(17120960924577811185)
XLA Ops:
  0.0 0.7 constant_dynamic-slice_fusion
  0.7 0.6 pad_maximum_fusion.refs_0_
  1.4 43.0 %shard_map.109 = bf16[32,64,256]{2,1,0:T(8,128)(2,1)} custom-call(bf16[64,256]{1,0:T(8,128)(2,1)} %pad_maximum_fusion.refs_0_), custom_call_target="tpu_custom_call" | custom-call | bytes 2097152 | tf_op jit(solution)/shard_map/pallas_call | solution.py:273
  44.4 1.3 fusion.32
  46.4 0.1 le.16
  46.5 0.8 select_reduce_fusion
  47.2 0.9 reshape.172
  48.1 0.0 copy-start.1
  48.1 1.8 fusion.35
  49.9 0.5 fusion.2
  50.4 0.0 copy-done.1
  50.4 0.0 copy-start.2
  50.4 0.0 copy-start.5
  50.4 0.0 copy-start.3
  50.5 0.8 fusion.4
  51.3 0.0 copy-done.2
  51.3 0.1 fusion.15
  51.4 0.6 pad.4.refs_0_
  52.0 9.9 %shard_map.110 = f32[8,8,128]{2,1,0:T(8,128)} custom-call(f32[8,128]{1,0:T(8,128)} %pad.4.refs_0_), custom_call_target="tpu_custom_call" | custom-call | bytes 65536 | tf_op jit(solution)/shard_map/pallas_call | solution.py:59
  61.9 0.8 reduce_sum.89
  62.7 0.0 copy-done.5
  62.7 0.1 fusion.17
  62.8 0.0 copy-done.3
  62.8 0.1 copy.31
  62.9 0.1 eq.55
  63.0 1.2 reduce-window.6
  64.2 0.2 slice_reduce_fusion
  64.5 0.1 eq.51
  64.6 0.1 fusion.21
  64.7 0.1 copy.30
  64.8 0.1 mul.90
  64.9 5.8 %scatter_custom_fusion = bf16[1024,512]{1,0:T(8,128)(2,1)} fusion(s32[512]{0:T(512)S(1)} %bitcast.57, bf16[64,512]{1,0:T(8,128)(2,1)S(1)} %fusion.17, s32[1024]{0:T(1024)S(1)} %pad_clamp_fusion.1, bf16[]{:T(256)} %constant.99.clone.1), kind=kCustom, calls=%fused_computation.20 | custom fusion | bytes 1048578 | tf_op jit(solution)/shard_map/scatter | solution.py:487
  70.7 69.3 %shard_map.111 = (bf16[8,2,64,768]{3,2,1,0:T(8,128)(2,1)}, bf16[8,2,64,768]{3,2,1,0:T(8,128)(2,1)}) custom-call(bf16[32,2,16,512]{3,2,1,0:T(8,128)(2,1)} %bitcast.52, bf16[2,512,768]{2,1,0:T(8,128)(2,1)} %refs_1_.2, bf16[2,512,768]{2,1,0:T(8,128)(2,1)} %refs_2_.1), custom_call_target="tpu_custom_call" | custom-call | flops 1610612736 | bytes 14680064 | tf_op jit(solution)/shard_map/pallas_call | solution.py:174
  140.1 0.0 copy-start
  140.1 1.8 convert_reduce_fusion
  141.9 0.1 copy-done
  141.9 0.2 convert_reduce_fusion.1
  142.2 0.8 multiply_convert_fusion.refs_0_
  143.0 82.8 %shard_map.112 = bf16[32,2,16,512]{3,2,1,0:T(8,128)(2,1)} custom-call(bf16[2,64,768]{2,1,0:T(8,128)(2,1)} %multiply_convert_fusion.refs_0_, bf16[2,768,512]{2,1,0:T(8,128)(2,1)} %refs_1_.3), custom_call_target="tpu_custom_call" | custom-call | flops 805306368 | bytes 6815744 | tf_op jit(solution)/shard_map/pallas_call | solution.py:379
  225.8 0.0 copy-start.4
  225.8 3.3 %gather_fusion = bf16[512,512]{1,0:T(8,128)(2,1)S(1)} fusion(bf16[1024,512]{1,0:T(8,128)(2,1)} %bitcast.49, s32[1024]{0:T(1024)S(1)} %pad_clamp_fusion), kind=kCustom, calls=%fused_computation.1 | custom fusion | bytes 1050624 | tf_op jit(solution)/shard_map/gather | solution.py:496
  229.2 0.0 copy-done.4
  229.2 0.1 copy.29
  229.2 0.4 fusion.5
  229.6 0.6 fusion.18
  (14 shorter events, 0.1 us)
Async XLA Ops:
  48.1 2.3 copy-start.1
  50.4 0.9 copy-start.2
  50.4 12.3 %copy-start.5 = (f32[512]{0:T(512)S(1)}, f32[512]{0:T(512)}, u32[]{:S(2)}) copy-start(f32[512]{0:T(512)} %param.16) | copy-start | bytes 6148
  50.4 12.3 %copy-start.3 = (s32[64,8]{0,1:T(8,128)S(1)}, s32[64,8]{0,1:T(8,128)}, u32[]{:S(2)}) copy-start(s32[64,8]{0,1:T(8,128)} %param.17) | copy-start | bytes 6148
  140.1 1.9 copy-start
  225.8 3.4 %copy-start.4 = (f32[64,8]{0,1:T(8,128)S(1)}, f32[64,8]{0,1:T(8,128)}, u32[]{:S(2)}) copy-start(f32[64,8]{0,1:T(8,128)} %param.18) | copy-start | bytes 6148

commit v5 on v4

--- a/solution.py
+++ b/solution.py
@@ -71,8 +71,8 @@
 
 
 def dispatch_reduce_kernel(n_ctx, n_exp, *refs):
-    (outgoing, gate_w, up_w, gate_recv, up_recv, incoming, gate_stage, up_stage,
-     d_send, d_recv, r_send, r_recv) = refs
+    (mixed, square_block, gain, slot_rows, gate_w, up_w, gate_recv, up_recv, square_all, outgoing, incoming,
+     gate_stage, up_stage, q_send, q_recv, d_send, d_recv, r_send, r_recv) = refs
     per_chunk = n_ctx // n_exp
     me_c = lax.axis_index("ctx")
     me_e = lax.axis_index("exp")
@@ -87,6 +87,29 @@
             barrier, inc=1, device_id={"exp": lax.rem(me_e + k, n_exp)}, device_id_type=MESH
         )
     pl.semaphore_wait(barrier, n_ctx + n_exp - 2)
+
+    def square_copy(r):
+        return pltpu.make_async_remote_copy(
+            src_ref=square_block,
+            dst_ref=square_all.at[me_e],
+            send_sem=q_send.at[r],
+            recv_sem=q_recv.at[me_e],
+            device_id={"exp": r},
+            device_id_type=MESH,
+        )
+
+    for k in range(1, n_exp):
+        square_copy(lax.rem(me_e + k, n_exp)).start()
+    pltpu.make_async_copy(square_block, square_all.at[me_e], q_recv.at[me_e]).start()
+    for s in range(n_exp):
+        pltpu.make_async_copy(square_all.at[s], square_all.at[s], q_recv.at[s]).wait()
+    square_sum = square_all[0]
+    for s in range(1, n_exp):
+        square_sum = square_sum + square_all[s]
+    scale = lax.rsqrt(square_sum[:, :1] / D + NORM_EPS)
+    normed = (mixed[...].astype(jnp.float32) * scale * gain[...]).astype(jnp.bfloat16)
+    filled = jnp.dot(slot_rows[...], normed, preferred_element_type=jnp.float32)
+    outgoing[...] = filled.astype(outgoing.dtype).reshape(outgoing.shape)
 
     def dispatch_copy(p):
         return pltpu.make_async_remote_copy(
@@ -163,23 +186,35 @@
         @pl.when(p != me_c)
         def _():
             dispatch_copy(p).wait_send()
-
-
-def dispatch_reduce(outgoing, gate_weight, up_weight, n_ctx, n_exp, collective_id):
+    for r in range(n_exp):
+
+        @pl.when(r != me_e)
+        def _():
+            square_copy(r).wait_send()
+
+
+def dispatch_reduce(
+    mixed, square_block, gain, slot_rows, out_shape, gate_weight, up_weight, n_ctx, n_exp, collective_id
+):
     hid = gate_weight.shape[-1]
-    slots = outgoing.shape[0] * outgoing.shape[2] // n_exp
+    size = math.prod(out_shape)
+    slots = out_shape[0] * out_shape[2] // n_exp
     recv_shape = jax.ShapeDtypeStruct((n_exp, EXP_ROW, slots, hid), jnp.bfloat16)
-    flops = 2 * 2 * outgoing.size * hid
-    nbytes = 2 * outgoing.size * 2 + 4 * gate_weight.size * 2 + 4 * n_exp * EXP_ROW * slots * hid * 2
+    flops = 2 * 2 * size * hid + 2 * size * mixed.shape[0]
+    nbytes = 2 * size * 2 + 4 * gate_weight.size * 2 + 4 * n_exp * EXP_ROW * slots * hid * 2
     return pl.pallas_call(
         functools.partial(dispatch_reduce_kernel, n_ctx, n_exp),
         out_shape=[recv_shape, recv_shape],
-        in_specs=[pl.BlockSpec(memory_space=pltpu.VMEM)] * 3,
+        in_specs=[pl.BlockSpec(memory_space=pltpu.VMEM)] * 6,
         out_specs=[pl.BlockSpec(memory_space=pltpu.VMEM)] * 2,
         scratch_shapes=[
-            pltpu.VMEM(outgoing.shape, outgoing.dtype),
+            pltpu.VMEM((n_exp,) + square_block.shape, jnp.float32),
+            pltpu.VMEM(out_shape, jnp.bfloat16),
+            pltpu.VMEM(out_shape, jnp.bfloat16),
             pltpu.VMEM(recv_shape.shape, jnp.bfloat16),
             pltpu.VMEM(recv_shape.shape, jnp.bfloat16),
+            pltpu.SemaphoreType.DMA((n_exp,)),
+            pltpu.SemaphoreType.DMA((n_exp,)),
             pltpu.SemaphoreType.DMA((n_ctx,)),
             pltpu.SemaphoreType.DMA((n_ctx,)),
             pltpu.SemaphoreType.DMA((n_exp, 2)),
@@ -187,7 +222,7 @@
         ],
         compiler_params=pltpu.CompilerParams(collective_id=collective_id, has_side_effects=True),
         cost_estimate=pl.CostEstimate(flops=flops, bytes_accessed=nbytes, transcendentals=0),
-    )(outgoing, gate_weight, up_weight)
+    )(mixed, square_block, gain, slot_rows, gate_weight, up_weight)
 
 
 def kv_gather_kernel(n_ctx, n_exp, group, *refs):
@@ -466,12 +501,7 @@
     mixed_rows = (residual.astype(jnp.float32) + attention.astype(jnp.float32)).astype(jnp.bfloat16)
     mixed_f = mixed_rows.astype(jnp.float32)
     square_part = jnp.sum(mixed_f * mixed_f, axis=1)
-    square_block = jnp.pad(square_part.reshape(1, shard_rows), ((0, 7), (0, 128 - shard_rows)))
-    (square_all,) = exchange([square_block], "exp", exp_count, True, 1)
-    square_sum = jnp.sum(square_all, axis=0)[0, :shard_rows]
-    normed = (mixed_f * lax.rsqrt(square_sum[:, None] / D + NORM_EPS) * norm_gain[None, :]).astype(
-        jnp.bfloat16
-    )
+    square_block = jnp.broadcast_to(square_part[:, None], (shard_rows, 128))
     expert_count = ctx_count * EXP_ROW
     capacity = 2 * shard_rows * TOPK // expert_count
     flat_ids = expert_ids.reshape(-1)
@@ -480,20 +510,30 @@
     )
     slot_rank = jnp.sum((jnp.cumsum(onehot, axis=0) - onehot) * onehot, axis=1)
     slot_index = flat_ids * capacity + slot_rank
-    source_rows = jnp.arange(shard_rows * TOPK, dtype=jnp.int32) // TOPK
-    outgoing = (
-        jnp.zeros((expert_count * capacity, normed.shape[1]), jnp.bfloat16)
-        .at[slot_index]
-        .set(normed[source_rows])
-    )
-    outgoing = outgoing.reshape(ctx_count, EXP_ROW, capacity, normed.shape[1])
-    gate_recv, up_recv = dispatch_reduce(outgoing, gate_weight, up_weight, ctx_count, exp_count, 2)
+    slot_total = expert_count * capacity
+    slot_rows = jnp.any(
+        slot_index.reshape(shard_rows, TOPK)[None, :, :]
+        == jnp.arange(slot_total, dtype=jnp.int32)[:, None, None],
+        axis=2,
+    ).astype(jnp.bfloat16)
+    gate_recv, up_recv = dispatch_reduce(
+        mixed_rows,
+        square_block,
+        norm_gain.reshape(1, -1),
+        slot_rows,
+        (ctx_count, EXP_ROW, capacity, mixed_rows.shape[1]),
+        gate_weight,
+        up_weight,
+        ctx_count,
+        exp_count,
+        2,
+    )
     gate_full = jnp.sum(gate_recv.astype(jnp.float32), axis=0)
     up_full = jnp.sum(up_recv.astype(jnp.float32), axis=0)
     hidden_mine = (jax.nn.silu(gate_full) * up_full).astype(jnp.bfloat16)
     returned = gather_return(hidden_mine, down_weight, ctx_count, exp_count, 4)
-    flat_back = returned.reshape(expert_count * capacity, normed.shape[1])
-    picked = flat_back[slot_index].astype(jnp.float32).reshape(shard_rows, TOPK, normed.shape[1])
+    flat_back = returned.reshape(expert_count * capacity, mixed_rows.shape[1])
+    picked = flat_back[slot_index].astype(jnp.float32).reshape(shard_rows, TOPK, mixed_rows.shape[1])
     routed_sum = jnp.sum(route_weight[:, :, None] * picked, axis=1)
     return (mixed_f + routed_sum).astype(jnp.bfloat16)
 

time: 231 us -> 219 us (0.948)
  the two profiles are of different devices: /device:TPU:64 before, /device:TPU:62 now
where the time goes in v5:
time: 219 us; the launch traced here: 218 us
  Pallas kernels  197 us (90%)
  other arithmetic  9.85 us (4%)
  local copies, waits for them, and re-layouts  7.56 us (3%)
  matrix products  2.6 us (1%)
    pallas_call x1, Pallas kernels, dispatch_reduce(): pl.pallas_call(functools.partial(dispatch_reduce_kernel, n_ctx, n_exp), o...  97.1 us
    pallas_call x1, Pallas kernels, gather_return(): pl.pallas_call(functools.partial(gather_return_kernel, n_ctx, n_exp), out...  62.3 us
    pallas_call x1, Pallas kernels, kv_gather(): pl.pallas_call(functools.partial(kv_gather_kernel, n_ctx, n_exp, group),...  38.1 us

profile of v5, /device:TPU:62, one launch (start us, length us, event | category | flops | bytes accessed | tf_op | source)
XLA Modules:
  0.0 218.3 jit_solution(1763982127055793591)
XLA Ops:
  0.0 0.7 constant_dynamic-slice_fusion
  0.7 0.6 pad_maximum_fusion.refs_0_
  1.4 38.1 %shard_map.109 = bf16[32,64,256]{2,1,0:T(8,128)(2,1)} custom-call(bf16[64,256]{1,0:T(8,128)(2,1)} %pad_maximum_fusion.refs_0_), custom_call_target="tpu_custom_call" | custom-call | bytes 2097152 | tf_op jit(solution)/shard_map/pallas_call | solution.py:308
  39.4 1.3 fusion.28
  41.4 0.1 le.16
  41.5 0.8 select_reduce_fusion
  42.3 0.9 reshape.116
  43.2 0.0 copy-start.1
  43.2 1.8 fusion.32
  45.0 0.5 fusion.3
  45.5 0.0 copy-done.1
  45.5 0.0 copy-start.3
  45.5 0.0 copy-start.4
  45.5 0.8 fusion.5
  46.3 0.1 copy.37
  46.4 0.0 copy-done.3
  46.4 0.8 fusion.13
  47.2 0.7 broadcast_in_dim.44.refs_1_
  47.8 0.0 copy-done.4
  47.8 0.1 copy.39
  47.9 0.1 eq.68
  48.0 1.2 reduce-window.6
  49.3 0.2 slice_reduce_fusion
  49.5 0.1 eq.64
  49.6 0.1 fusion.18
  49.7 0.1 reduce_sum.81
  49.9 0.7 fusion.2
  50.6 0.9 copy.43.refs_3_
  51.4 97.1 %shard_map.110 = (bf16[8,2,64,768]{3,2,1,0:T(8,128)(2,1)}, bf16[8,2,64,768]{3,2,1,0:T(8,128)(2,1)}) custom-call(bf16[64,512]{1,0:T(8,128)(2,1)} %get-tuple-element.10.refs_0_, f32[64,128]{1,0:T(8,128)} %broadcast_in_dim.44.refs_1_, f32[1,512]{1,0:T(1,128)} %bitcast.52, bf16[1024,64]{1,0:T(8,128)(2,1)} %copy.43.refs_3_, bf16[2,512,768]{2,1,0:T(8,128)(2,1)} %refs_4_.1, ...), custom_call_target="tpu_custom_call" | custom-call | flops 1677721600 | bytes 14680064 | tf_op jit(solution)/shard_map/pallas_call | solution.py:205
  148.5 0.0 copy-start
  148.5 1.8 convert_reduce_fusion
  150.3 0.1 copy-done
  150.4 0.2 convert_reduce_fusion.1
  150.6 0.8 multiply_convert_fusion.refs_0_
  151.4 62.3 %shard_map.111 = bf16[32,2,16,512]{3,2,1,0:T(8,128)(2,1)} custom-call(bf16[2,64,768]{2,1,0:T(8,128)(2,1)} %multiply_convert_fusion.refs_0_, bf16[2,768,512]{2,1,0:T(8,128)(2,1)} %refs_1_.1), custom_call_target="tpu_custom_call" | custom-call | flops 805306368 | bytes 6815744 | tf_op jit(solution)/shard_map/pallas_call | solution.py:414
  213.7 0.1 mul.80
  213.8 0.0 copy-start.5
  213.8 0.0 copy-start.2
  213.8 3.4 %gather_fusion = bf16[512,512]{1,0:T(8,128)(2,1)S(1)} fusion(bf16[1024,512]{1,0:T(8,128)(2,1)} %bitcast.43, s32[1024]{0:T(1024)S(1)} %pad_clamp_fusion), kind=kCustom, calls=%fused_computation | custom fusion | bytes 1050624 | tf_op jit(solution)/shard_map/gather | solution.py:536
  217.2 0.0 copy-done.5
  217.2 0.1 copy.38
  217.3 0.4 fusion.6
  217.7 0.0 copy-done.2
  217.7 0.6 fusion.14
  (12 shorter events, 0.1 us)
Async XLA Ops:
  43.2 2.3 %copy-start.1 = (bf16[32,64,256]{2,1,0:T(8,128)(2,1)S(1)}, bf16[32,64,256]{2,1,0:T(8,128)(2,1)}, u32[]{:S(2)}) copy-start(bf16[32,64,256]{2,1,0:T(8,128)(2,1)} %shard_map.109) | copy-start | bytes 3145732
  45.5 0.9 copy-start.3
  45.5 2.4 %copy-start.4 = (s32[64,8]{0,1:T(8,128)S(1)}, s32[64,8]{0,1:T(8,128)}, u32[]{:S(2)}) copy-start(s32[64,8]{0,1:T(8,128)} %param.17) | copy-start | bytes 6148
  148.5 1.9 copy-start
  213.8 3.4 %copy-start.5 = (f32[64,8]{0,1:T(8,128)S(1)}, f32[64,8]{0,1:T(8,128)}, u32[]{:S(2)}) copy-start(f32[64,8]{0,1:T(8,128)} %param.18) | copy-start | bytes 6148
  213.8 3.9 %copy-start.2 = (bf16[64,512]{1,0:T(8,128)(2,1)S(1)}, bf16[64,512]{1,0:T(8,128)(2,1)}, u32[]{:S(2)}) copy-start(bf16[64,512]{1,0:T(8,128)(2,1)} %get-tuple-element.10.refs_0_) | copy-start | bytes 196612

commit v6 on v5

--- a/solution.py
+++ b/solution.py
@@ -18,6 +18,7 @@
 MASKED_SCORE = -1e30
 NORM_EPS = 1e-06
 MESH = pl.DeviceIdType.MESH
+AHEAD = 2
 
 
 def exchange_kernel(axis, n, gather, n_in, *refs):
@@ -121,7 +122,7 @@
             device_id_type=MESH,
         )
 
-    for t in range(n_exp):
+    def dispatch_wave(t):
         z_r = lax.rem(plane + 2 * n_exp - me_e - t, n_exp)
         for y in range(per_chunk):
             p = z_r * per_chunk + y
@@ -133,6 +134,9 @@
             @pl.when(p == me_c)
             def _():
                 pltpu.make_async_copy(outgoing.at[p], incoming.at[p], d_recv.at[p]).start()
+
+    for t in range(AHEAD):
+        dispatch_wave(t)
 
     parts = ((gate_w, gate_stage, gate_recv), (up_w, up_stage, up_recv))
 
@@ -170,6 +174,9 @@
         def _():
             for which, (_, stage, recv) in enumerate(parts):
                 pltpu.make_async_copy(stage.at[j], recv.at[j], r_recv.at[j, which]).start()
+
+        if t + AHEAD < n_exp:
+            dispatch_wave(t + AHEAD)
 
     for s in range(n_exp):
         for which, (_, _, recv) in enumerate(parts):
@@ -348,7 +355,7 @@
             device_id_type=MESH,
         )
 
-    for t in range(n_exp):
+    def gather_wave(t):
         r = lax.rem(me_e + 2 * n_exp - plane - t, n_exp)
 
         @pl.when(r != me_e)
@@ -358,6 +365,9 @@
         @pl.when(r == me_e)
         def _():
             pltpu.make_async_copy(hidden_mine, hidden_all.at[r], a_recv.at[r]).start()
+
+    for t in range(AHEAD):
+        gather_wave(t)
 
     def return_copy(s):
         return pltpu.make_async_remote_copy(
@@ -389,6 +399,9 @@
             @pl.when(s == me_c)
             def _():
                 pltpu.make_async_copy(ret_stage.at[s], returned.at[s], b_recv.at[s]).start()
+
+        if t + AHEAD < n_exp:
+            gather_wave(t + AHEAD)
 
     for s in range(n_ctx):
         pltpu.make_async_copy(returned.at[s], returned.at[s], b_recv.at[s]).wait()

time: 219 us -> 239 us (1.091)
  the two profiles are of different devices: /device:TPU:62 before, /device:TPU:112 now
where the time goes in v6:
time: 239 us
  Pallas kernels  218 us (91%)
  other arithmetic  9.85 us (4%)
  local copies, waits for them, and re-layouts  7.56 us (3%)
  matrix products  2.59 us (1%)
    pallas_call x1, Pallas kernels, dispatch_reduce(): pl.pallas_call(functools.partial(dispatch_reduce_kernel, n_ctx, n_exp), o...  99.5 us
    pallas_call x1, Pallas kernels, gather_return(): pl.pallas_call(functools.partial(gather_return_kernel, n_ctx, n_exp), out...  82.5 us
    pallas_call x1, Pallas kernels, kv_gather(): pl.pallas_call(functools.partial(kv_gather_kernel, n_ctx, n_exp, group),...  35.8 us

profile of v6, /device:TPU:112, one launch (start us, length us, event | category | flops | bytes accessed | tf_op | source)
XLA Modules:
  0.0 238.7 jit_solution(3691444187920604516)
XLA Ops:
  0.0 0.7 constant_dynamic-slice_fusion
  0.7 0.6 pad_maximum_fusion.refs_0_
  1.4 35.8 %shard_map.109 = bf16[32,64,256]{2,1,0:T(8,128)(2,1)} custom-call(bf16[64,256]{1,0:T(8,128)(2,1)} %pad_maximum_fusion.refs_0_), custom_call_target="tpu_custom_call" | custom-call | bytes 2097152 | tf_op jit(solution)/shard_map/pallas_call | solution.py:315
  37.2 1.3 fusion.28
  39.2 0.1 le.16
  39.3 0.8 select_reduce_fusion
  40.0 0.9 reshape.116
  40.9 0.0 copy-start.1
  40.9 1.8 fusion.32
  42.7 0.5 fusion.3
  43.2 0.0 copy-done.1
  43.2 0.0 copy-start.3
  43.2 0.0 copy-start.4
  43.2 0.8 fusion.5
  44.1 0.1 copy.37
  44.1 0.0 copy-done.3
  44.1 0.8 fusion.13
  44.9 0.7 broadcast_in_dim.44.refs_1_
  45.6 0.0 copy-done.4
  45.6 0.1 copy.39
  45.7 0.1 eq.68
  45.8 1.2 reduce-window.6
  47.0 0.2 slice_reduce_fusion
  47.3 0.1 eq.64
  47.4 0.1 fusion.18
  47.5 0.1 reduce_sum.81
  47.6 0.7 fusion.2
  48.3 0.9 copy.43.refs_3_
  49.2 99.5 %shard_map.110 = (bf16[8,2,64,768]{3,2,1,0:T(8,128)(2,1)}, bf16[8,2,64,768]{3,2,1,0:T(8,128)(2,1)}) custom-call(bf16[64,512]{1,0:T(8,128)(2,1)} %get-tuple-element.10.refs_0_, f32[64,128]{1,0:T(8,128)} %broadcast_in_dim.44.refs_1_, f32[1,512]{1,0:T(1,128)} %bitcast.52, bf16[1024,64]{1,0:T(8,128)(2,1)} %copy.43.refs_3_, bf16[2,512,768]{2,1,0:T(8,128)(2,1)} %refs_4_.1, ...), custom_call_target="tpu_custom_call" | custom-call | flops 1677721600 | bytes 14680064 | tf_op jit(solution)/shard_map/pallas_call | solution.py:212
  148.7 0.0 copy-start
  148.7 1.8 convert_reduce_fusion
  150.5 0.1 copy-done
  150.6 0.2 convert_reduce_fusion.1
  150.8 0.8 multiply_convert_fusion.refs_0_
  151.6 82.5 %shard_map.111 = bf16[32,2,16,512]{3,2,1,0:T(8,128)(2,1)} custom-call(bf16[2,64,768]{2,1,0:T(8,128)(2,1)} %multiply_convert_fusion.refs_0_, bf16[2,768,512]{2,1,0:T(8,128)(2,1)} %refs_1_.1), custom_call_target="tpu_custom_call" | custom-call | flops 805306368 | bytes 6815744 | tf_op jit(solution)/shard_map/pallas_call | solution.py:427
  234.1 0.1 mul.80
  234.2 0.0 copy-start.5
  234.2 0.0 copy-start.2
  234.2 3.4 %gather_fusion = bf16[512,512]{1,0:T(8,128)(2,1)S(1)} fusion(bf16[1024,512]{1,0:T(8,128)(2,1)} %bitcast.43, s32[1024]{0:T(1024)S(1)} %pad_clamp_fusion), kind=kCustom, calls=%fused_computation | custom fusion | bytes 1050624 | tf_op jit(solution)/shard_map/gather | solution.py:549
  237.6 0.0 copy-done.5
  237.6 0.1 copy.38
  237.7 0.4 fusion.6
  238.1 0.0 copy-done.2
  238.1 0.6 fusion.14
  (12 shorter events, 0.1 us)
Async XLA Ops:
  40.9 2.3 copy-start.1
  43.2 0.9 copy-start.3
  43.2 2.4 copy-start.4
  148.7 1.9 copy-start
  234.2 3.4 %copy-start.5 = (f32[64,8]{0,1:T(8,128)S(1)}, f32[64,8]{0,1:T(8,128)}, u32[]{:S(2)}) copy-start(f32[64,8]{0,1:T(8,128)} %param.18) | copy-start | bytes 6148
  234.2 3.9 %copy-start.2 = (bf16[64,512]{1,0:T(8,128)(2,1)S(1)}, bf16[64,512]{1,0:T(8,128)(2,1)}, u32[]{:S(2)}) copy-start(bf16[64,512]{1,0:T(8,128)(2,1)} %get-tuple-element.10.refs_0_) | copy-start | bytes 196612

commit v7 on v3

--- a/solution.py
+++ b/solution.py
@@ -70,9 +70,10 @@
     )(*xs)
 
 
-def dispatch_reduce_kernel(n_ctx, n_exp, *refs):
-    (outgoing, gate_w, up_w, gate_recv, up_recv, incoming, gate_stage, up_stage,
-     d_send, d_recv, r_send, r_recv) = refs
+def moe_kernel(n_ctx, n_exp, *refs):
+    (mixed, square_block, gain, slot_rows, gate_w, up_w, down_w, w_hi, w_lo, out,
+     square_all, outgoing, incoming, gate_stage, up_stage, gate_recv, up_recv, hidden_mine, hidden_all, ret_stage,
+     returned, q_send, q_recv, d_send, d_recv, r_send, r_recv, a_send, a_recv, b_send, b_recv) = refs
     per_chunk = n_ctx // n_exp
     me_c = lax.axis_index("ctx")
     me_e = lax.axis_index("exp")
@@ -87,6 +88,30 @@
             barrier, inc=1, device_id={"exp": lax.rem(me_e + k, n_exp)}, device_id_type=MESH
         )
     pl.semaphore_wait(barrier, n_ctx + n_exp - 2)
+
+    def square_copy(r):
+        return pltpu.make_async_remote_copy(
+            src_ref=square_block,
+            dst_ref=square_all.at[me_e],
+            send_sem=q_send.at[r],
+            recv_sem=q_recv.at[me_e],
+            device_id={"exp": r},
+            device_id_type=MESH,
+        )
+
+    for k in range(1, n_exp):
+        square_copy(lax.rem(me_e + k, n_exp)).start()
+    pltpu.make_async_copy(square_block, square_all.at[me_e], q_recv.at[me_e]).start()
+    for s in range(n_exp):
+        pltpu.make_async_copy(square_all.at[s], square_all.at[s], q_recv.at[s]).wait()
+    square_sum = square_all[0]
+    for s in range(1, n_exp):
+        square_sum = square_sum + square_all[s]
+    scale = lax.rsqrt(square_sum[:, :1] / D + NORM_EPS)
+    mixed_f = mixed[...].astype(jnp.float32)
+    normed = (mixed_f * scale * gain[...]).astype(jnp.bfloat16)
+    filled = jnp.dot(slot_rows[...], normed, preferred_element_type=jnp.float32)
+    outgoing[...] = filled.astype(outgoing.dtype).reshape(outgoing.shape)
 
     def dispatch_copy(p):
         return pltpu.make_async_remote_copy(
@@ -151,44 +176,129 @@
     for s in range(n_exp):
         for which, (_, _, recv) in enumerate(parts):
             pltpu.make_async_copy(recv.at[s], recv.at[s], r_recv.at[s, which]).wait()
-    for j in range(n_exp):
-
-        @pl.when(j != me_e)
+    gate_sum = gate_recv[0].astype(jnp.float32)
+    up_sum = up_recv[0].astype(jnp.float32)
+    for s in range(1, n_exp):
+        gate_sum = gate_sum + gate_recv[s].astype(jnp.float32)
+        up_sum = up_sum + up_recv[s].astype(jnp.float32)
+    hidden_mine[...] = (gate_sum / (1.0 + jnp.exp(-gate_sum)) * up_sum).astype(hidden_mine.dtype)
+
+    def gather_copy(r):
+        return pltpu.make_async_remote_copy(
+            src_ref=hidden_mine,
+            dst_ref=hidden_all.at[me_e],
+            send_sem=a_send.at[r],
+            recv_sem=a_recv.at[me_e],
+            device_id={"exp": r},
+            device_id_type=MESH,
+        )
+
+    for t in range(n_exp):
+        r = lax.rem(me_e + 2 * n_exp - plane - t, n_exp)
+
+        @pl.when(r != me_e)
         def _():
+            gather_copy(r).start()
+
+        @pl.when(r == me_e)
+        def _():
+            pltpu.make_async_copy(hidden_mine, hidden_all.at[r], a_recv.at[r]).start()
+
+    def return_copy(s):
+        return pltpu.make_async_remote_copy(
+            src_ref=ret_stage.at[s],
+            dst_ref=returned.at[me_c],
+            send_sem=b_send.at[s],
+            recv_sem=b_recv.at[me_c],
+            device_id={"ctx": s},
+            device_id_type=MESH,
+        )
+
+    for t in range(n_exp):
+        j = lax.rem(me_e + plane + t, n_exp)
+        pltpu.make_async_copy(hidden_all.at[j], hidden_all.at[j], a_recv.at[j]).wait()
+        first = pl.multiple_of(j * per_chunk, per_chunk)
+        for k in range(EXP_ROW):
+            res = jnp.dot(hidden_all[j, k], down_w[k], preferred_element_type=jnp.float32)
+            ret_stage[pl.ds(first, per_chunk), k] = res.astype(ret_stage.dtype).reshape(
+                per_chunk, rows // per_chunk, res.shape[-1]
+            )
+        for y in range(per_chunk):
+            s = j * per_chunk + y
+
+            @pl.when(s != me_c)
+            def _():
+                return_copy(s).start()
+
+            @pl.when(s == me_c)
+            def _():
+                pltpu.make_async_copy(ret_stage.at[s], returned.at[s], b_recv.at[s]).start()
+
+    for s in range(n_ctx):
+        pltpu.make_async_copy(returned.at[s], returned.at[s], b_recv.at[s]).wait()
+    back = returned[...].reshape(w_hi.shape[1], returned.shape[-1])
+    routed = jnp.dot(w_hi[...], back, preferred_element_type=jnp.float32) + jnp.dot(
+        w_lo[...], back, preferred_element_type=jnp.float32
+    )
+    out[...] = (mixed_f + routed).astype(out.dtype)
+
+    for r in range(n_exp):
+
+        @pl.when(r != me_e)
+        def _():
+            gather_copy(r).wait_send()
+            square_copy(r).wait_send()
             for which in range(2):
-                reduce_copy(j, which).wait_send()
+                reduce_copy(r, which).wait_send()
 
     for p in range(n_ctx):
 
         @pl.when(p != me_c)
         def _():
             dispatch_copy(p).wait_send()
-
-
-def dispatch_reduce(outgoing, gate_weight, up_weight, n_ctx, n_exp, collective_id):
+            return_copy(p).wait_send()
+
+
+def moe(mixed, square_block, gain, slot_rows, out_shape, gate_weight, up_weight, down_weight, w_hi, w_lo,
+        n_ctx, n_exp, collective_id):
     hid = gate_weight.shape[-1]
-    slots = outgoing.shape[0] * outgoing.shape[2] // n_exp
-    recv_shape = jax.ShapeDtypeStruct((n_exp, EXP_ROW, slots, hid), jnp.bfloat16)
-    flops = 2 * 2 * outgoing.size * hid
-    nbytes = 2 * outgoing.size * 2 + 4 * gate_weight.size * 2 + 4 * n_exp * EXP_ROW * slots * hid * 2
+    size = math.prod(out_shape)
+    slots = out_shape[0] * out_shape[2] // n_exp
+    recv_shape = (n_exp, EXP_ROW, slots, hid)
+    flops = 2 * 3 * size * hid + 2 * size * mixed.shape[0] * 3
+    nbytes = 4 * size * 2 + 6 * gate_weight.size * 2 + 8 * n_exp * EXP_ROW * slots * hid * 2
+    vmem = pltpu.VMEM
     return pl.pallas_call(
-        functools.partial(dispatch_reduce_kernel, n_ctx, n_exp),
-        out_shape=[recv_shape, recv_shape],
-        in_specs=[pl.BlockSpec(memory_space=pltpu.VMEM)] * 3,
-        out_specs=[pl.BlockSpec(memory_space=pltpu.VMEM)] * 2,
+        functools.partial(moe_kernel, n_ctx, n_exp),
+        out_shape=jax.ShapeDtypeStruct(mixed.shape, jnp.bfloat16),
+        in_specs=[pl.BlockSpec(memory_space=pltpu.VMEM)] * 9,
+        out_specs=pl.BlockSpec(memory_space=pltpu.VMEM),
         scratch_shapes=[
-            pltpu.VMEM(outgoing.shape, outgoing.dtype),
-            pltpu.VMEM(recv_shape.shape, jnp.bfloat16),
-            pltpu.VMEM(recv_shape.shape, jnp.bfloat16),
+            vmem((n_exp,) + square_block.shape, jnp.float32),
+            vmem(out_shape, jnp.bfloat16),
+            vmem(out_shape, jnp.bfloat16),
+            vmem(recv_shape, jnp.bfloat16),
+            vmem(recv_shape, jnp.bfloat16),
+            vmem(recv_shape, jnp.bfloat16),
+            vmem(recv_shape, jnp.bfloat16),
+            vmem(recv_shape[1:], jnp.bfloat16),
+            vmem(recv_shape, jnp.bfloat16),
+            vmem(out_shape, jnp.bfloat16),
+            vmem(out_shape, jnp.bfloat16),
+            pltpu.SemaphoreType.DMA((n_exp,)),
+            pltpu.SemaphoreType.DMA((n_exp,)),
             pltpu.SemaphoreType.DMA((n_ctx,)),
             pltpu.SemaphoreType.DMA((n_ctx,)),
             pltpu.SemaphoreType.DMA((n_exp, 2)),
             pltpu.SemaphoreType.DMA((n_exp, 2)),
+            pltpu.SemaphoreType.DMA((n_exp,)),
+            pltpu.SemaphoreType.DMA((n_exp,)),
+            pltpu.SemaphoreType.DMA((n_ctx,)),
+            pltpu.SemaphoreType.DMA((n_ctx,)),
         ],
         compiler_params=pltpu.CompilerParams(collective_id=collective_id, has_side_effects=True),
         cost_estimate=pl.CostEstimate(flops=flops, bytes_accessed=nbytes, transcendentals=0),
-    )(outgoing, gate_weight, up_weight)
-
+    )(mixed, square_block, gain, slot_rows, gate_weight, up_weight, down_weight, w_hi, w_lo)
 
 def kv_gather_kernel(n_ctx, n_exp, group, *refs):
     block, kv_all, s1_send, s1_recv, s2_send, s2_recv = refs
@@ -358,12 +468,7 @@
     mixed_rows = (residual.astype(jnp.float32) + attention.astype(jnp.float32)).astype(jnp.bfloat16)
     mixed_f = mixed_rows.astype(jnp.float32)
     square_part = jnp.sum(mixed_f * mixed_f, axis=1)
-    square_block = jnp.pad(square_part.reshape(1, shard_rows), ((0, 7), (0, 128 - shard_rows)))
-    (square_all,) = exchange([square_block], "exp", exp_count, True, 1)
-    square_sum = jnp.sum(square_all, axis=0)[0, :shard_rows]
-    normed = (mixed_f * lax.rsqrt(square_sum[:, None] / D + NORM_EPS) * norm_gain[None, :]).astype(
-        jnp.bfloat16
-    )
+    square_block = jnp.broadcast_to(square_part[:, None], (shard_rows, 128))
     expert_count = ctx_count * EXP_ROW
     capacity = 2 * shard_rows * TOPK // expert_count
     flat_ids = expert_ids.reshape(-1)
@@ -372,33 +477,38 @@
     )
     slot_rank = jnp.sum((jnp.cumsum(onehot, axis=0) - onehot) * onehot, axis=1)
     slot_index = flat_ids * capacity + slot_rank
-    source_rows = jnp.arange(shard_rows * TOPK, dtype=jnp.int32) // TOPK
-    outgoing = (
-        jnp.zeros((expert_count * capacity, normed.shape[1]), jnp.bfloat16)
-        .at[slot_index]
-        .set(normed[source_rows])
-    )
-    outgoing = outgoing.reshape(ctx_count, EXP_ROW, capacity, normed.shape[1])
-    gate_recv, up_recv = dispatch_reduce(outgoing, gate_weight, up_weight, ctx_count, exp_count, 2)
-    gate_full = jnp.sum(gate_recv.astype(jnp.float32), axis=0)
-    up_full = jnp.sum(up_recv.astype(jnp.float32), axis=0)
-    hidden_mine = (jax.nn.silu(gate_full) * up_full).astype(jnp.bfloat16)
-    (hidden,) = exchange([hidden_mine], "exp", exp_count, True, 4)
-    expert_out = jnp.einsum(
-        "jksh,khd->jksd", hidden, down_weight, preferred_element_type=jnp.float32
+    slot_total = expert_count * capacity
+    slot_rows = jnp.any(
+        slot_index.reshape(shard_rows, TOPK)[None, :, :]
+        == jnp.arange(slot_total, dtype=jnp.int32)[:, None, None],
+        axis=2,
     ).astype(jnp.bfloat16)
-    per_chunk = ctx_count // exp_count
-    expert_out = (
-        expert_out.reshape(exp_count, EXP_ROW, per_chunk, capacity, normed.shape[1])
-        .transpose(0, 2, 1, 3, 4)
-        .reshape(ctx_count, EXP_ROW, capacity, normed.shape[1])
-    )
-    (returned,) = exchange([expert_out], "ctx", ctx_count, False, 5)
-    flat_back = returned.reshape(expert_count * capacity, normed.shape[1])
-    picked = flat_back[slot_index].astype(jnp.float32).reshape(shard_rows, TOPK, normed.shape[1])
-    routed_sum = jnp.sum(route_weight[:, :, None] * picked, axis=1)
-    return (mixed_f + routed_sum).astype(jnp.bfloat16)
-
+    slot_weight = jnp.sum(
+        jnp.where(
+            slot_index.reshape(shard_rows, TOPK)[:, :, None]
+            == jnp.arange(slot_total, dtype=jnp.int32)[None, None, :],
+            route_weight[:, :, None],
+            0.0,
+        ),
+        axis=1,
+    )
+    w_hi = slot_weight.astype(jnp.bfloat16)
+    w_lo = (slot_weight - w_hi.astype(jnp.float32)).astype(jnp.bfloat16)
+    return moe(
+        mixed_rows,
+        square_block,
+        norm_gain.reshape(1, -1),
+        slot_rows,
+        (ctx_count, EXP_ROW, capacity, mixed_rows.shape[1]),
+        gate_weight,
+        up_weight,
+        down_weight,
+        w_hi,
+        w_lo,
+        ctx_count,
+        exp_count,
+        2,
+    )
 
 def solution(mesh):
     placed = (

time: 255 us -> 208 us (0.82)
  the two profiles are of different devices: /device:TPU:48 before, /device:TPU:4 now
where the time goes in v7:
time: 208 us
  Pallas kernels  191 us (92%)
  other arithmetic  7.48 us (4%)
  local copies, waits for them, and re-layouts  5.59 us (3%)
  matrix products  2.59 us (1%)
    pallas_call x1, Pallas kernels, moe(): pl.pallas_call(functools.partial(moe_kernel, n_ctx, n_exp), out_shape=jax...  146 us
    pallas_call x1, Pallas kernels, kv_gather(): pl.pallas_call(functools.partial(kv_gather_kernel, n_ctx, n_exp, group),...  45.4 us

profile of v7, /device:TPU:4, one launch (start us, length us, event | category | flops | bytes accessed | tf_op | source)
XLA Modules:
  0.0 207.9 jit_solution(11324318511867428125)
XLA Ops:
  0.0 0.7 constant_dynamic-slice_fusion
  0.7 0.6 pad_maximum_fusion.refs_0_
  1.4 45.4 %shard_map.109 = bf16[32,64,256]{2,1,0:T(8,128)(2,1)} custom-call(bf16[64,256]{1,0:T(8,128)(2,1)} %pad_maximum_fusion.refs_0_), custom_call_target="tpu_custom_call" | custom-call | bytes 2097152 | tf_op jit(solution)/shard_map/pallas_call | solution.py:383
  46.8 1.3 fusion.25
  48.7 0.1 le.16
  48.8 0.8 select_reduce_fusion.1
  49.6 0.9 reshape.87
  50.5 0.0 copy-start
  50.5 1.8 fusion.28
  52.3 0.5 fusion.3
  52.8 0.0 copy-done
  52.8 0.0 copy-start.1
  52.8 0.0 copy-start.2
  52.8 0.0 copy-start.3
  52.8 0.8 fusion.5
  53.7 0.1 copy.41
  53.7 0.0 copy-done.1
  53.7 0.8 multiply_reduce_fusion
  54.5 0.7 broadcast_in_dim.56.refs_1_
  55.2 0.0 copy-done.2
  55.2 0.1 copy.42
  55.3 0.1 eq.81
  55.4 1.2 reduce-window.6
  56.6 0.2 slice_reduce_fusion
  56.9 0.1 eq.77
  56.9 0.1 fusion.15
  57.1 0.1 reduce_sum.61
  57.2 0.1 copy.45
  57.2 0.1 copy.46
  57.3 0.0 copy-done.3
  57.3 0.1 copy.48
  57.4 0.7 select_reduce_fusion
  58.1 0.7 subtract_convert_fusion
  58.9 0.7 fusion.2
  59.6 0.8 copy.49.refs_3_
  60.4 146.0 %shard_map.110 = bf16[64,512]{1,0:T(8,128)(2,1)} custom-call(bf16[64,512]{1,0:T(8,128)(2,1)} %get-tuple-element.8.refs_0_, f32[64,128]{1,0:T(8,128)} %broadcast_in_dim.56.refs_1_, f32[1,512]{1,0:T(1,128)} %bitcast.43, bf16[1024,64]{1,0:T(8,128)(2,1)} %copy.49.refs_3_, bf16[2,512,768]{2,1,0:T(8,128)(2,1)} %refs_4_.1, bf16[2,512,768]{2,1,0:T(8,128)(2,1)} %refs_5_.1, ...), custom_call_target="tpu_custom_call" | custom-call | flops 2617245696 | bytes 26214400 | tf_op jit(solution)/shard_map/pallas_call | solution.py:271
  206.4 1.5 copy.56
  (10 shorter events, 0.1 us)
Async XLA Ops:
  50.5 2.3 %copy-start = (bf16[32,64,256]{2,1,0:T(8,128)(2,1)S(1)}, bf16[32,64,256]{2,1,0:T(8,128)(2,1)}, u32[]{:S(2)}) copy-start(bf16[32,64,256]{2,1,0:T(8,128)(2,1)} %shard_map.109) | copy-start | bytes 3145732
  52.8 0.9 copy-start.1
  52.8 2.4 %copy-start.2 = (s32[64,8]{0,1:T(8,128)S(1)}, s32[64,8]{0,1:T(8,128)}, u32[]{:S(2)}) copy-start(s32[64,8]{0,1:T(8,128)} %param.17) | copy-start | bytes 6148
  52.8 4.5 %copy-start.3 = (f32[64,8]{0,1:T(8,128)S(1)}, f32[64,8]{0,1:T(8,128)}, u32[]{:S(2)}) copy-start(f32[64,8]{0,1:T(8,128)} %param.18) | copy-start | bytes 6148

commit v8 on v7

--- a/solution.py
+++ b/solution.py
@@ -71,9 +71,10 @@
 
 
 def moe_kernel(n_ctx, n_exp, *refs):
-    (mixed, square_block, gain, slot_rows, gate_w, up_w, down_w, w_hi, w_lo, out,
-     square_all, outgoing, incoming, gate_stage, up_stage, gate_recv, up_recv, hidden_mine, hidden_all, ret_stage,
-     returned, q_send, q_recv, d_send, d_recv, r_send, r_recv, a_send, a_recv, b_send, b_recv) = refs
+    (queries, kv_block, residual, query_pos, key_pos, gain, slot_rows, gate_w, up_w, down_w, w_hi, w_lo, out,
+     kv_all, mixed, square_block, square_all, outgoing, incoming, gate_stage, up_stage, gate_recv, up_recv,
+     hidden_mine, hidden_all, ret_stage, returned, s1_send, s1_recv, s2_send, s2_recv, q_send, q_recv, d_send,
+     d_recv, r_send, r_recv, a_send, a_recv, b_send, b_recv) = refs
     per_chunk = n_ctx // n_exp
     me_c = lax.axis_index("ctx")
     me_e = lax.axis_index("exp")
@@ -88,6 +89,85 @@
             barrier, inc=1, device_id={"exp": lax.rem(me_e + k, n_exp)}, device_id_type=MESH
         )
     pl.semaphore_wait(barrier, n_ctx + n_exp - 2)
+
+    group = QUERY_HEADS // KEY_VALUE_HEADS // (queries.shape[1] // HEAD_SIZE)
+    q = lax.rem(me_e, group)
+    head_base = me_e - q
+    planes = n_exp
+    halves = 2
+
+    def first_copy(p):
+        return pltpu.make_async_remote_copy(
+            src_ref=kv_block,
+            dst_ref=kv_all.at[me_c],
+            send_sem=s1_send.at[p],
+            recv_sem=s1_recv.at[me_c],
+            device_id={"ctx": p},
+            device_id_type=MESH,
+        )
+
+    for h in range(halves):
+        z_r = lax.rem(plane + 2 * planes - q - h * (planes // halves), planes)
+        for y in range(per_chunk):
+            p = z_r * per_chunk + y
+
+            @pl.when(p != me_c)
+            def _():
+                first_copy(p).start()
+
+            @pl.when(p == me_c)
+            def _():
+                pltpu.make_async_copy(kv_block, kv_all.at[p], s1_recv.at[p]).start()
+
+    def second_copy(h, r):
+        first = pl.multiple_of(lax.rem(plane + q + h * (planes // halves), planes) * per_chunk, per_chunk)
+        return pltpu.make_async_remote_copy(
+            src_ref=kv_all.at[pl.ds(first, per_chunk)],
+            dst_ref=kv_all.at[pl.ds(first, per_chunk)],
+            send_sem=s2_send.at[r, h],
+            recv_sem=s2_recv.at[r, h],
+            device_id={"exp": head_base + lax.rem(q + r, group)},
+            device_id_type=MESH,
+        )
+
+    for h in range(halves):
+        z_s = lax.rem(plane + q + h * (planes // halves), planes)
+        for y in range(per_chunk):
+            s = z_s * per_chunk + y
+            pltpu.make_async_copy(kv_all.at[s], kv_all.at[s], s1_recv.at[s]).wait()
+        for r in range(1, group):
+            second_copy(h, r).start()
+    for h in range(halves):
+        for r in range(1, group):
+            second_copy(h, r).wait_recv()
+
+    total_rows = kv_all.shape[0] * kv_all.shape[1]
+    keys = kv_all[:, :, :HEAD_SIZE].reshape(total_rows, HEAD_SIZE)
+    values = kv_all[:, :, HEAD_SIZE:].reshape(total_rows, HEAD_SIZE)
+    visible = key_pos[...] <= query_pos[...]
+    inv_scale = 1.0 / math.sqrt(HEAD_SIZE)
+    square_part = jnp.zeros((queries.shape[0], 1), jnp.float32)
+    for h in range(queries.shape[1] // HEAD_SIZE):
+        cols = slice(h * HEAD_SIZE, (h + 1) * HEAD_SIZE)
+        scores = (
+            lax.dot_general(
+                queries[:, cols], keys, (((1,), (1,)), ((), ())), preferred_element_type=jnp.float32
+            )
+            * inv_scale
+        )
+        scores = jnp.where(visible, scores, MASKED_SCORE)
+        newest = jnp.max(scores, axis=1, keepdims=True)
+        weights = jnp.where(visible, jnp.exp(scores - newest), 0.0)
+        weight_sum = jnp.sum(weights, axis=1, keepdims=True)
+        weighted = jnp.dot(weights.astype(jnp.bfloat16), values, preferred_element_type=jnp.float32)
+        attention = (weighted / weight_sum).astype(jnp.bfloat16)
+        mixed_h = (residual[:, cols].astype(jnp.float32) + attention.astype(jnp.float32)).astype(
+            jnp.bfloat16
+        )
+        mixed[:, cols] = mixed_h
+        mixed_hf = mixed_h.astype(jnp.float32)
+        square_part = square_part + jnp.sum(mixed_hf * mixed_hf, axis=1, keepdims=True)
+    square_block[...] = jnp.broadcast_to(square_part, square_block.shape)
 
     def square_copy(r):
         return pltpu.make_async_remote_copy(
@@ -258,9 +338,23 @@
             dispatch_copy(p).wait_send()
             return_copy(p).wait_send()
 
-
-def moe(mixed, square_block, gain, slot_rows, out_shape, gate_weight, up_weight, down_weight, w_hi, w_lo,
-        n_ctx, n_exp, collective_id):
+    for h in range(halves):
+        for r in range(1, group):
+            second_copy(h, r).wait_send()
+    for h in range(halves):
+        z_r = lax.rem(plane + 2 * planes - q - h * (planes // halves), planes)
+        for y in range(per_chunk):
+            p = z_r * per_chunk + y
+
+            @pl.when(p != me_c)
+            def _():
+                first_copy(p).wait_send()
+
+
+def moe(queries, kv_block, residual, query_pos, key_pos, gain, slot_rows, out_shape, gate_weight, up_weight,
+        down_weight, w_hi, w_lo, n_ctx, n_exp, collective_id):
+    mixed = residual
+    square_shape = (residual.shape[0], 128)
     hid = gate_weight.shape[-1]
     size = math.prod(out_shape)
     slots = out_shape[0] * out_shape[2] // n_exp
@@ -271,10 +365,13 @@
     return pl.pallas_call(
         functools.partial(moe_kernel, n_ctx, n_exp),
         out_shape=jax.ShapeDtypeStruct(mixed.shape, jnp.bfloat16),
-        in_specs=[pl.BlockSpec(memory_space=pltpu.VMEM)] * 9,
+        in_specs=[pl.BlockSpec(memory_space=pltpu.VMEM)] * 12,
         out_specs=pl.BlockSpec(memory_space=pltpu.VMEM),
         scratch_shapes=[
-            vmem((n_exp,) + square_block.shape, jnp.float32),
+            vmem((n_ctx,) + kv_block.shape, jnp.bfloat16),
+            vmem(residual.shape, jnp.bfloat16),
+            vmem(square_shape, jnp.float32),
+            vmem((n_exp,) + square_shape, jnp.float32),
             vmem(out_shape, jnp.bfloat16),
             vmem(out_shape, jnp.bfloat16),
             vmem(recv_shape, jnp.bfloat16),
@@ -285,8 +382,6 @@
             vmem(recv_shape, jnp.bfloat16),
             vmem(out_shape, jnp.bfloat16),
             vmem(out_shape, jnp.bfloat16),
-            pltpu.SemaphoreType.DMA((n_exp,)),
-            pltpu.SemaphoreType.DMA((n_exp,)),
             pltpu.SemaphoreType.DMA((n_ctx,)),
             pltpu.SemaphoreType.DMA((n_ctx,)),
             pltpu.SemaphoreType.DMA((n_exp, 2)),
@@ -295,10 +390,17 @@
             pltpu.SemaphoreType.DMA((n_exp,)),
             pltpu.SemaphoreType.DMA((n_ctx,)),
             pltpu.SemaphoreType.DMA((n_ctx,)),
+            pltpu.SemaphoreType.DMA((n_exp, 2)),
+            pltpu.SemaphoreType.DMA((n_exp, 2)),
+            pltpu.SemaphoreType.DMA((n_exp,)),
+            pltpu.SemaphoreType.DMA((n_exp,)),
+            pltpu.SemaphoreType.DMA((n_ctx,)),
+            pltpu.SemaphoreType.DMA((n_ctx,)),
         ],
         compiler_params=pltpu.CompilerParams(collective_id=collective_id, has_side_effects=True),
         cost_estimate=pl.CostEstimate(flops=flops, bytes_accessed=nbytes, transcendentals=0),
-    )(mixed, square_block, gain, slot_rows, gate_weight, up_weight, down_weight, w_hi, w_lo)
+    )(queries, kv_block, residual, query_pos, key_pos, gain, slot_rows, gate_weight, up_weight, down_weight,
+      w_hi, w_lo)
 
 def kv_gather_kernel(n_ctx, n_exp, group, *refs):
     block, kv_all, s1_send, s1_recv, s2_send, s2_recv = refs
@@ -421,54 +523,14 @@
     block_ids = jnp.arange(ctx_count, dtype=jnp.int32)
     own_block = jnp.sum(jnp.where(block_ids == ctx_index, block_order, 0))
     local_rows = jnp.arange(shard_rows, dtype=jnp.int32)
-    query_pos = jnp.tile(own_block * shard_rows + local_rows, local_head)
-    query_flat = (
-        queries.reshape(shard_rows, local_head, HEAD_SIZE)
-        .transpose(1, 0, 2)
-        .reshape(local_head * shard_rows, HEAD_SIZE)
-    )
-    inv_scale = 1.0 / math.sqrt(HEAD_SIZE)
-    key_value_all = kv_gather(
-        jnp.concatenate([my_keys, my_values], axis=1),
-        ctx_count,
-        exp_count,
-        QUERY_HEADS // KEY_VALUE_HEADS // local_head,
-        0,
-    )
-    key_value_all = key_value_all.reshape(ctx_count * shard_rows, 2 * HEAD_SIZE)
-    piece_keys = key_value_all[:, :HEAD_SIZE]
-    piece_values = key_value_all[:, HEAD_SIZE:]
-    key_index = jnp.arange(piece_keys.shape[0], dtype=jnp.int32)
+    query_pos = (own_block * shard_rows + local_rows).reshape(shard_rows, 1)
+    key_index = jnp.arange(ctx_count * shard_rows, dtype=jnp.int32)
     owner_shard = key_index // shard_rows
     key_block = jnp.sum(
         jnp.where(owner_shard[:, None] == block_ids[None, :], block_order[None, :], 0), axis=1
     )
-    key_pos = key_block * shard_rows + key_index % shard_rows
-    visible = key_pos[None, :] <= query_pos[:, None]
-    scores = (
-        lax.dot_general(
-            query_flat, piece_keys, (((1,), (1,)), ((), ())), preferred_element_type=jnp.float32
-        )
-        * inv_scale
-    )
-    scores = jnp.where(visible, scores, MASKED_SCORE)
-    newest = jnp.max(scores, axis=1)
-    weights = jnp.where(visible, jnp.exp(scores - newest[:, None]), 0.0)
-    running_sum = jnp.sum(weights, axis=1)
-    weighted = jnp.dot(
-        weights.astype(jnp.bfloat16), piece_values, preferred_element_type=jnp.float32
-    )
-    attention = (
-        (weighted / running_sum[:, None])
-        .reshape(local_head, shard_rows, HEAD_SIZE)
-        .transpose(1, 0, 2)
-        .reshape(shard_rows, local_head * HEAD_SIZE)
-        .astype(jnp.bfloat16)
-    )
-    mixed_rows = (residual.astype(jnp.float32) + attention.astype(jnp.float32)).astype(jnp.bfloat16)
-    mixed_f = mixed_rows.astype(jnp.float32)
-    square_part = jnp.sum(mixed_f * mixed_f, axis=1)
-    square_block = jnp.broadcast_to(square_part[:, None], (shard_rows, 128))
+    key_pos = (key_block * shard_rows + key_index % shard_rows).reshape(1, -1)
+    kv_block = jnp.concatenate([my_keys, my_values], axis=1)
     expert_count = ctx_count * EXP_ROW
     capacity = 2 * shard_rows * TOPK // expert_count
     flat_ids = expert_ids.reshape(-1)
@@ -495,11 +557,14 @@
     w_hi = slot_weight.astype(jnp.bfloat16)
     w_lo = (slot_weight - w_hi.astype(jnp.float32)).astype(jnp.bfloat16)
     return moe(
-        mixed_rows,
-        square_block,
+        queries,
+        kv_block,
+        residual,
+        query_pos,
+        key_pos,
         norm_gain.reshape(1, -1),
         slot_rows,
-        (ctx_count, EXP_ROW, capacity, mixed_rows.shape[1]),
+        (ctx_count, EXP_ROW, capacity, residual.shape[1]),
         gate_weight,
         up_weight,
         down_weight,

time: 208 us -> 181 us (0.87)
  the two profiles are of different devices: /device:TPU:4 before, /device:TPU:96 now
where the time goes in v8:
time: 181 us; the launch traced here: 180 us
  Pallas kernels  167 us (92%)
  other arithmetic  6.89 us (4%)
  local copies, waits for them, and re-layouts  5.25 us (3%)
    pallas_call x1, Pallas kernels, moe(): pl.pallas_call(functools.partial(moe_kernel, n_ctx, n_exp), out_shape=jax...  167 us

profile of v8, /device:TPU:96, one launch (start us, length us, event | category | flops | bytes accessed | tf_op | source)
XLA Modules:
  0.0 180.3 jit_solution(3776170562006366560)
XLA Ops:
  0.0 0.0 copy-start
  0.0 0.7 constant_dynamic-slice_fusion
  0.8 0.6 pad_maximum_fusion.refs_1_
  1.4 0.8 copy.28
  2.1 0.1 eq.81
  2.3 1.2 reduce-window.6
  3.5 0.2 slice_reduce_fusion
  3.7 0.1 eq.77
  3.8 0.1 fusion.3
  4.0 0.1 reduce_sum.41
  4.0 0.1 copy.31
  4.1 0.7 multiply_add_fusion
  4.8 0.1 copy.32
  4.9 0.8 copy.34
  5.7 0.7 select_reduce_fusion
  6.4 0.7 subtract_convert_fusion
  7.1 0.7 fusion
  7.8 0.8 copy.35.refs_6_
  8.7 0.0 copy-done
  8.7 0.7 fusion.9
  10.1 0.6 iota_add_fusion.refs_3_
  10.7 0.1 select_reduce_fusion.1
  10.8 0.6 fusion.5.refs_4_
  11.4 167.4 %shard_map.109 = bf16[64,512]{1,0:T(8,128)(2,1)} custom-call(bf16[64,512]{1,0:T(8,128)(2,1)} %refs_0_.1, bf16[64,256]{1,0:T(8,128)(2,1)} %pad_maximum_fusion.refs_1_, bf16[64,512]{1,0:T(8,128)(2,1)} %refs_2_.1, s32[64,1]{1,0:T(8,128)} %iota_add_fusion.refs_3_, s32[1,2048]{1,0:T(1,128)} %fusion.5.refs_4_, f32[1,512]{1,0:T(1,128)} %bitcast.22, ...), custom_call_target="tpu_custom_call" | custom-call | flops 2617245696 | bytes 26214400 | tf_op jit(solution)/shard_map/pallas_call | solution.py:365
  178.8 1.5 copy.39
  (6 shorter events, 0.1 us)
Async XLA Ops:
  0.0 8.7 %copy-start = (s32[32]{0:T(128)S(1)}, s32[32]{0:T(128)}, u32[]{:S(2)}) copy-start(s32[32]{0:T(128)} %param.14) | copy-start | bytes 388

commit v9 on v8

--- a/solution.py
+++ b/solution.py
@@ -18,6 +18,7 @@
 MASKED_SCORE = -1e30
 NORM_EPS = 1e-06
 MESH = pl.DeviceIdType.MESH
+Y_LO = 2
 
 
 def exchange_kernel(axis, n, gather, n_in, *refs):
@@ -73,8 +74,8 @@
 def moe_kernel(n_ctx, n_exp, *refs):
     (queries, kv_block, residual, query_pos, key_pos, gain, slot_rows, gate_w, up_w, down_w, w_hi, w_lo, out,
      kv_all, mixed, square_block, square_all, outgoing, incoming, gate_stage, up_stage, gate_recv, up_recv,
-     hidden_mine, hidden_all, ret_stage, returned, s1_send, s1_recv, s2_send, s2_recv, q_send, q_recv, d_send,
-     d_recv, r_send, r_recv, a_send, a_recv, b_send, b_recv) = refs
+     hidden_mine, hidden_all, ret_stage, returned, column_sum, partner_sum, s1_send, s1_recv, s2_send, s2_recv,
+     q_send, q_recv, d_send, d_recv, r_send, r_recv, a_send, a_recv, b_send, b_recv, p_sem) = refs
     per_chunk = n_ctx // n_exp
     me_c = lax.axis_index("ctx")
     me_e = lax.axis_index("exp")
@@ -217,15 +218,17 @@
                 pltpu.make_async_copy(outgoing.at[p], incoming.at[p], d_recv.at[p]).start()
 
     parts = ((gate_w, gate_stage, gate_recv), (up_w, up_stage, up_recv))
+    mx = me_e // Y_LO
+    my = lax.rem(me_e, Y_LO)
 
     def reduce_copy(j, which):
         _, stage, recv = parts[which]
         return pltpu.make_async_remote_copy(
             src_ref=stage.at[j],
-            dst_ref=recv.at[me_e],
-            send_sem=r_send.at[j, which],
-            recv_sem=r_recv.at[me_e, which],
-            device_id={"exp": j},
+            dst_ref=recv.at[mx, lax.rem(j, Y_LO)],
+            send_sem=r_send.at[j // Y_LO, lax.rem(j, Y_LO), which],
+            recv_sem=r_recv.at[mx, lax.rem(j, Y_LO), which],
+            device_id={"exp": (j // Y_LO) * Y_LO + my},
             device_id_type=MESH,
         )
 
@@ -243,24 +246,41 @@
                     stage.dtype
                 )
 
-        @pl.when(j != me_e)
+        @pl.when(j // Y_LO != mx)
         def _():
             for which in range(2):
                 reduce_copy(j, which).start()
 
-        @pl.when(j == me_e)
+        @pl.when(j // Y_LO == mx)
         def _():
             for which, (_, stage, recv) in enumerate(parts):
-                pltpu.make_async_copy(stage.at[j], recv.at[j], r_recv.at[j, which]).start()
-
-    for s in range(n_exp):
+                pltpu.make_async_copy(
+                    stage.at[j], recv.at[mx, lax.rem(j, Y_LO)], r_recv.at[mx, lax.rem(j, Y_LO), which]
+                ).start()
+
+    n_x = n_exp // Y_LO
+    for sx in range(n_x):
+        for cy in range(Y_LO):
+            for which, (_, _, recv) in enumerate(parts):
+                pltpu.make_async_copy(recv.at[sx, cy], recv.at[sx, cy], r_recv.at[sx, cy, which]).wait()
+    for cy in range(Y_LO):
         for which, (_, _, recv) in enumerate(parts):
-            pltpu.make_async_copy(recv.at[s], recv.at[s], r_recv.at[s, which]).wait()
-    gate_sum = gate_recv[0].astype(jnp.float32)
-    up_sum = up_recv[0].astype(jnp.float32)
-    for s in range(1, n_exp):
-        gate_sum = gate_sum + gate_recv[s].astype(jnp.float32)
-        up_sum = up_sum + up_recv[s].astype(jnp.float32)
+            total = recv[0, cy].astype(jnp.float32)
+            for sx in range(1, n_x):
+                total = total + recv[sx, cy].astype(jnp.float32)
+            column_sum[cy, which] = total
+    partner_copy = pltpu.make_async_remote_copy(
+        src_ref=column_sum.at[Y_LO - 1 - my],
+        dst_ref=partner_sum,
+        send_sem=p_sem.at[0],
+        recv_sem=p_sem.at[1],
+        device_id={"exp": mx * Y_LO + Y_LO - 1 - my},
+        device_id_type=MESH,
+    )
+    partner_copy.start()
+    partner_copy.wait_recv()
+    gate_sum = column_sum[my, 0] + partner_sum[0]
+    up_sum = column_sum[my, 1] + partner_sum[1]
     hidden_mine[...] = (gate_sum / (1.0 + jnp.exp(-gate_sum)) * up_sum).astype(hidden_mine.dtype)
 
     def gather_copy(r):
@@ -328,8 +348,13 @@
         def _():
             gather_copy(r).wait_send()
             square_copy(r).wait_send()
+
+        @pl.when(r // Y_LO != mx)
+        def _():
             for which in range(2):
                 reduce_copy(r, which).wait_send()
+
+    partner_copy.wait_send()
 
     for p in range(n_ctx):
 
@@ -359,6 +384,7 @@
     size = math.prod(out_shape)
     slots = out_shape[0] * out_shape[2] // n_exp
     recv_shape = (n_exp, EXP_ROW, slots, hid)
+    column_shape = (n_exp // Y_LO, Y_LO, EXP_ROW, slots, hid)
     flops = 2 * 3 * size * hid + 2 * size * mixed.shape[0] * 3
     nbytes = 4 * size * 2 + 6 * gate_weight.size * 2 + 8 * n_exp * EXP_ROW * slots * hid * 2
     vmem = pltpu.VMEM
@@ -376,12 +402,14 @@
             vmem(out_shape, jnp.bfloat16),
             vmem(recv_shape, jnp.bfloat16),
             vmem(recv_shape, jnp.bfloat16),
-            vmem(recv_shape, jnp.bfloat16),
-            vmem(recv_shape, jnp.bfloat16),
+            vmem(column_shape, jnp.bfloat16),
+            vmem(column_shape, jnp.bfloat16),
             vmem(recv_shape[1:], jnp.bfloat16),
             vmem(recv_shape, jnp.bfloat16),
             vmem(out_shape, jnp.bfloat16),
             vmem(out_shape, jnp.bfloat16),
+            vmem((Y_LO, 2) + recv_shape[1:], jnp.float32),
+            vmem((2,) + recv_shape[1:], jnp.float32),
             pltpu.SemaphoreType.DMA((n_ctx,)),
             pltpu.SemaphoreType.DMA((n_ctx,)),
             pltpu.SemaphoreType.DMA((n_exp, 2)),
@@ -390,12 +418,13 @@
             pltpu.SemaphoreType.DMA((n_exp,)),
             pltpu.SemaphoreType.DMA((n_ctx,)),
             pltpu.SemaphoreType.DMA((n_ctx,)),
-            pltpu.SemaphoreType.DMA((n_exp, 2)),
-            pltpu.SemaphoreType.DMA((n_exp, 2)),
+            pltpu.SemaphoreType.DMA((n_exp // Y_LO, Y_LO, 2)),
+            pltpu.SemaphoreType.DMA((n_exp // Y_LO, Y_LO, 2)),
             pltpu.SemaphoreType.DMA((n_exp,)),
             pltpu.SemaphoreType.DMA((n_exp,)),
             pltpu.SemaphoreType.DMA((n_ctx,)),
             pltpu.SemaphoreType.DMA((n_ctx,)),
+            pltpu.SemaphoreType.DMA((2,)),
         ],
         compiler_params=pltpu.CompilerParams(collective_id=collective_id, has_side_effects=True),
         cost_estimate=pl.CostEstimate(flops=flops, bytes_accessed=nbytes, transcendentals=0),

time: 181 us -> 190 us (1.050)
  the two profiles are of different devices: /device:TPU:96 before, /device:TPU:24 now
where the time goes in v9:
time: 190 us
  Pallas kernels  177 us (93%)
  other arithmetic  6.89 us (4%)
  local copies, waits for them, and re-layouts  5.25 us (3%)
    pallas_call x1, Pallas kernels, moe(): pl.pallas_call(functools.partial(moe_kernel, n_ctx, n_exp), out_shape=jax...  177 us

profile of v9, /device:TPU:24, one launch (start us, length us, event | category | flops | bytes accessed | tf_op | source)
XLA Modules:
  0.0 190.0 jit_solution(6031740281258406359)
XLA Ops:
  0.0 0.0 copy-start
  0.0 0.7 constant_dynamic-slice_fusion
  0.8 0.6 pad_maximum_fusion.refs_1_
  1.4 0.8 copy.28
  2.1 0.1 eq.81
  2.3 1.2 reduce-window.6
  3.5 0.2 slice_reduce_fusion
  3.7 0.1 eq.77
  3.8 0.1 fusion.3
  4.0 0.1 reduce_sum.41
  4.0 0.1 copy.31
  4.1 0.7 multiply_add_fusion
  4.8 0.1 copy.32
  4.9 0.8 copy.34
  5.7 0.7 select_reduce_fusion
  6.4 0.7 subtract_convert_fusion
  7.1 0.7 fusion
  7.8 0.8 copy.35.refs_6_
  8.7 0.0 copy-done
  8.7 0.7 fusion.9
  10.1 0.6 iota_add_fusion.refs_3_
  10.7 0.1 select_reduce_fusion.1
  10.8 0.6 fusion.5.refs_4_
  11.4 177.1 %shard_map.109 = bf16[64,512]{1,0:T(8,128)(2,1)} custom-call(bf16[64,512]{1,0:T(8,128)(2,1)} %refs_0_.1, bf16[64,256]{1,0:T(8,128)(2,1)} %pad_maximum_fusion.refs_1_, bf16[64,512]{1,0:T(8,128)(2,1)} %refs_2_.1, s32[64,1]{1,0:T(8,128)} %iota_add_fusion.refs_3_, s32[1,2048]{1,0:T(1,128)} %fusion.5.refs_4_, f32[1,512]{1,0:T(1,128)} %bitcast.22, ...), custom_call_target="tpu_custom_call" | custom-call | flops 2617245696 | bytes 26214400 | tf_op jit(solution)/shard_map/pallas_call | solution.py:391
  188.5 1.5 copy.39
  (6 shorter events, 0.1 us)
Async XLA Ops:
  0.0 8.7 %copy-start = (s32[32]{0:T(128)S(1)}, s32[32]{0:T(128)}, u32[]{:S(2)}) copy-start(s32[32]{0:T(128)} %param.14) | copy-start | bytes 388

commit v10 on v8

--- a/solution.py
+++ b/solution.py
@@ -71,8 +71,8 @@
 
 
 def moe_kernel(n_ctx, n_exp, *refs):
-    (queries, kv_block, residual, query_pos, key_pos, gain, slot_rows, gate_w, up_w, down_w, w_hi, w_lo, out,
-     kv_all, mixed, square_block, square_all, outgoing, incoming, gate_stage, up_stage, gate_recv, up_recv,
+    (queries, key_rows, value_rows, residual, block_order, gain, slot_rows, gate_w, up_w, down_w, w_hi, w_lo, out,
+     kv_block, kv_all, mixed, square_block, square_all, outgoing, incoming, gate_stage, up_stage, gate_recv, up_recv,
      hidden_mine, hidden_all, ret_stage, returned, s1_send, s1_recv, s2_send, s2_recv, q_send, q_recv, d_send,
      d_recv, r_send, r_recv, a_send, a_recv, b_send, b_recv) = refs
     per_chunk = n_ctx // n_exp
@@ -91,6 +91,9 @@
     pl.semaphore_wait(barrier, n_ctx + n_exp - 2)
 
     group = QUERY_HEADS // KEY_VALUE_HEADS // (queries.shape[1] // HEAD_SIZE)
+    head_cols = pl.ds(pl.multiple_of((me_e // group) * HEAD_SIZE, HEAD_SIZE), HEAD_SIZE)
+    kv_block[:, :HEAD_SIZE] = key_rows[:, head_cols]
+    kv_block[:, HEAD_SIZE:] = value_rows[:, head_cols]
     q = lax.rem(me_e, group)
     head_base = me_e - q
     planes = n_exp
@@ -144,7 +147,13 @@
     total_rows = kv_all.shape[0] * kv_all.shape[1]
     keys = kv_all[:, :, :HEAD_SIZE].reshape(total_rows, HEAD_SIZE)
     values = kv_all[:, :, HEAD_SIZE:].reshape(total_rows, HEAD_SIZE)
-    visible = key_pos[...] <= query_pos[...]
+    block_rows = kv_all.shape[1]
+    query_pos = block_order[me_c] * block_rows + lax.broadcasted_iota(jnp.int32, (queries.shape[0], 1), 0)
+    key_lane = lax.broadcasted_iota(jnp.int32, (1, total_rows), 1)
+    key_pos = key_lane % block_rows
+    for b in range(kv_all.shape[0]):
+        key_pos = jnp.where(key_lane // block_rows == b, key_pos + block_order[b] * block_rows, key_pos)
+    visible = key_pos <= query_pos
     inv_scale = 1.0 / math.sqrt(HEAD_SIZE)
     square_part = jnp.zeros((queries.shape[0], 1), jnp.float32)
     for h in range(queries.shape[1] // HEAD_SIZE):
@@ -351,8 +360,9 @@
                 first_copy(p).wait_send()
 
 
-def moe(queries, kv_block, residual, query_pos, key_pos, gain, slot_rows, out_shape, gate_weight, up_weight,
+def moe(queries, key_rows, value_rows, residual, block_order, gain, slot_rows, out_shape, gate_weight, up_weight,
         down_weight, w_hi, w_lo, n_ctx, n_exp, collective_id):
+    kv_shape = (residual.shape[0], KEY_VALUE_HEADS * HEAD_SIZE)
     mixed = residual
     square_shape = (residual.shape[0], 128)
     hid = gate_weight.shape[-1]
@@ -365,10 +375,13 @@
     return pl.pallas_call(
         functools.partial(moe_kernel, n_ctx, n_exp),
         out_shape=jax.ShapeDtypeStruct(mixed.shape, jnp.bfloat16),
-        in_specs=[pl.BlockSpec(memory_space=pltpu.VMEM)] * 12,
+        in_specs=[pl.BlockSpec(memory_space=pltpu.VMEM)] * 4
+        + [pl.BlockSpec(memory_space=pltpu.SMEM)]
+        + [pl.BlockSpec(memory_space=pltpu.VMEM)] * 7,
         out_specs=pl.BlockSpec(memory_space=pltpu.VMEM),
         scratch_shapes=[
-            vmem((n_ctx,) + kv_block.shape, jnp.bfloat16),
+            vmem(kv_shape, jnp.bfloat16),
+            vmem((n_ctx,) + kv_shape, jnp.bfloat16),
             vmem(residual.shape, jnp.bfloat16),
             vmem(square_shape, jnp.float32),
             vmem((n_exp,) + square_shape, jnp.float32),
@@ -399,7 +412,7 @@
         ],
         compiler_params=pltpu.CompilerParams(collective_id=collective_id, has_side_effects=True),
         cost_estimate=pl.CostEstimate(flops=flops, bytes_accessed=nbytes, transcendentals=0),
-    )(queries, kv_block, residual, query_pos, key_pos, gain, slot_rows, gate_weight, up_weight, down_weight,
+    )(queries, key_rows, value_rows, residual, block_order, gain, slot_rows, gate_weight, up_weight, down_weight,
       w_hi, w_lo)
 
 def kv_gather_kernel(n_ctx, n_exp, group, *refs):
@@ -517,20 +530,6 @@
     local_head = queries.shape[1] // HEAD_SIZE
     expert_index = lax.axis_index("exp")
     ctx_index = lax.axis_index("ctx")
-    key_value_head = expert_index * local_head // (QUERY_HEADS // KEY_VALUE_HEADS)
-    my_keys = lax.dynamic_slice_in_dim(key_rows, key_value_head * HEAD_SIZE, HEAD_SIZE, 1)
-    my_values = lax.dynamic_slice_in_dim(value_head_rows, key_value_head * HEAD_SIZE, HEAD_SIZE, 1)
-    block_ids = jnp.arange(ctx_count, dtype=jnp.int32)
-    own_block = jnp.sum(jnp.where(block_ids == ctx_index, block_order, 0))
-    local_rows = jnp.arange(shard_rows, dtype=jnp.int32)
-    query_pos = (own_block * shard_rows + local_rows).reshape(shard_rows, 1)
-    key_index = jnp.arange(ctx_count * shard_rows, dtype=jnp.int32)
-    owner_shard = key_index // shard_rows
-    key_block = jnp.sum(
-        jnp.where(owner_shard[:, None] == block_ids[None, :], block_order[None, :], 0), axis=1
-    )
-    key_pos = (key_block * shard_rows + key_index % shard_rows).reshape(1, -1)
-    kv_block = jnp.concatenate([my_keys, my_values], axis=1)
     expert_count = ctx_count * EXP_ROW
     capacity = 2 * shard_rows * TOPK // expert_count
     flat_ids = expert_ids.reshape(-1)
@@ -558,10 +557,10 @@
     w_lo = (slot_weight - w_hi.astype(jnp.float32)).astype(jnp.bfloat16)
     return moe(
         queries,
-        kv_block,
+        key_rows,
+        value_head_rows,
         residual,
-        query_pos,
-        key_pos,
+        block_order,
         norm_gain.reshape(1, -1),
         slot_rows,
         (ctx_count, EXP_ROW, capacity, residual.shape[1]),

time: 181 us -> 179 us (0.989)
  Pallas kernels: 167 us -> 170 us
  other arithmetic: 6.89 us -> 4.23 us
    pallas_call x1, Pallas kernels: 167 us -> 170 us  [moe(): pl.pallas_call(functools.partial(moe_kernel, n_ctx, n_exp), out_shape=jax...]
where the time goes in v10:
time: 179 us
  Pallas kernels  170 us (95%)
  local copies, waits for them, and re-layouts  4.5 us (3%)
  other arithmetic  4.23 us (2%)
    pallas_call x1, Pallas kernels, moe(): pl.pallas_call(functools.partial(moe_kernel, n_ctx, n_exp), out_shape=jax...  170 us

profile of v10, /device:TPU:96, one launch (start us, length us, event | category | flops | bytes accessed | tf_op | source)
XLA Modules:
  0.0 178.8 jit_solution(732428180656005578)
XLA Ops:
  0.0 0.8 copy.28
  0.8 0.1 eq.55
  0.9 1.2 reduce-window.6
  2.1 0.2 slice_reduce_fusion
  2.4 0.1 eq.51
  2.5 0.1 fusion.3
  2.6 0.1 reduce_sum.21
  2.7 0.1 copy.31
  2.7 0.7 multiply_add_fusion
  3.4 0.1 copy.32
  3.5 0.8 copy.34
  4.3 0.7 select_reduce_fusion
  5.0 0.7 subtract_convert_fusion
  5.8 0.7 fusion
  6.5 0.8 copy.35.refs_6_
  7.3 170.0 %shard_map.109 = bf16[64,512]{1,0:T(8,128)(2,1)} custom-call(bf16[64,512]{1,0:T(8,128)(2,1)} %refs_0_.1, bf16[64,256]{1,0:T(8,128)(2,1)} %refs_1_.1, bf16[64,256]{1,0:T(8,128)(2,1)} %refs_2_.1, bf16[64,512]{1,0:T(8,128)(2,1)} %refs_3_.1, s32[32]{0:T(128)} %refs_4_.1, f32[1,512]{1,0:T(1,128)} %bitcast.20, bf16[1024,64]{1,0:T(8,128)(2,1)} %copy.35.refs_6_, ...), custom_call_target="tpu_custom_call" | custom-call | flops 2617245696 | bytes 26214400 | tf_op jit(solution)/shard_map/pallas_call | solution.py:375
  177.3 1.5 copy.39
  (4 shorter events, 0.1 us)

commit v11 on v10

--- a/solution.py
+++ b/solution.py
@@ -71,8 +71,8 @@
 
 
 def moe_kernel(n_ctx, n_exp, *refs):
-    (queries, key_rows, value_rows, residual, block_order, gain, slot_rows, gate_w, up_w, down_w, w_hi, w_lo, out,
-     kv_block, kv_all, mixed, square_block, square_all, outgoing, incoming, gate_stage, up_stage, gate_recv, up_recv,
+    (queries, key_rows, value_rows, residual, block_order, gain, expert_ids, route_weight, gate_w, up_w, down_w, out,
+     slot_rows, w_hi, w_lo, kv_block, kv_all, mixed, square_block, square_all, outgoing, incoming, gate_stage, up_stage, gate_recv, up_recv,
      hidden_mine, hidden_all, ret_stage, returned, s1_send, s1_recv, s2_send, s2_recv, q_send, q_recv, d_send,
      d_recv, r_send, r_recv, a_send, a_recv, b_send, b_recv) = refs
     per_chunk = n_ctx // n_exp
@@ -132,6 +132,36 @@
             device_id={"exp": head_base + lax.rem(q + r, group)},
             device_id_type=MESH,
         )
+
+    rows_here, topk = expert_ids.shape
+    slot_total = slot_rows.shape[1]
+    capacity = slot_total // (n_ctx * EXP_ROW)
+    ids = expert_ids[...]
+    expert_lane = lax.broadcasted_iota(jnp.int32, (rows_here, n_ctx * EXP_ROW), 1)
+    picks = [(ids[:, i : i + 1] == expert_lane).astype(jnp.float32) for i in range(topk)]
+    per_row = picks[0]
+    for i in range(1, topk):
+        per_row = per_row + picks[i]
+    earlier = (
+        lax.broadcasted_iota(jnp.int32, (rows_here, rows_here), 1)
+        < lax.broadcasted_iota(jnp.int32, (rows_here, rows_here), 0)
+    ).astype(jnp.bfloat16)
+    before = jnp.dot(earlier, per_row.astype(jnp.bfloat16), preferred_element_type=jnp.float32)
+    slot_lane = lax.broadcasted_iota(jnp.int32, (rows_here, slot_total), 1)
+    chosen = jnp.zeros((rows_here, slot_total), jnp.float32)
+    weight = jnp.zeros((rows_here, slot_total), jnp.float32)
+    weights_in = route_weight[...]
+    for i in range(topk):
+        rank = jnp.sum(picks[i] * before, axis=1, keepdims=True)
+        before = before + picks[i]
+        slot = ids[:, i : i + 1] * capacity + rank.astype(jnp.int32)
+        hit = slot == slot_lane
+        chosen = jnp.where(hit, 1.0, chosen)
+        weight = jnp.where(hit, weights_in[:, i : i + 1], weight)
+    slot_rows[...] = chosen.astype(slot_rows.dtype)
+    high = weight.astype(jnp.bfloat16)
+    w_hi[...] = high
+    w_lo[...] = (weight - high.astype(jnp.float32)).astype(jnp.bfloat16)
 
     for h in range(halves):
         z_s = lax.rem(plane + q + h * (planes // halves), planes)
@@ -199,7 +229,9 @@
     scale = lax.rsqrt(square_sum[:, :1] / D + NORM_EPS)
     mixed_f = mixed[...].astype(jnp.float32)
     normed = (mixed_f * scale * gain[...]).astype(jnp.bfloat16)
-    filled = jnp.dot(slot_rows[...], normed, preferred_element_type=jnp.float32)
+    filled = lax.dot_general(
+        slot_rows[...], normed, (((0,), (0,)), ((), ())), preferred_element_type=jnp.float32
+    )
     outgoing[...] = filled.astype(outgoing.dtype).reshape(outgoing.shape)
 
     def dispatch_copy(p):
@@ -360,8 +392,9 @@
                 first_copy(p).wait_send()
 
 
-def moe(queries, key_rows, value_rows, residual, block_order, gain, slot_rows, out_shape, gate_weight, up_weight,
-        down_weight, w_hi, w_lo, n_ctx, n_exp, collective_id):
+def moe(queries, key_rows, value_rows, residual, block_order, gain, expert_ids, route_weight, out_shape, gate_weight,
+        up_weight, down_weight, n_ctx, n_exp, collective_id):
+    slot_total = out_shape[0] * out_shape[1] * out_shape[2]
     kv_shape = (residual.shape[0], KEY_VALUE_HEADS * HEAD_SIZE)
     mixed = residual
     square_shape = (residual.shape[0], 128)
@@ -377,9 +410,12 @@
         out_shape=jax.ShapeDtypeStruct(mixed.shape, jnp.bfloat16),
         in_specs=[pl.BlockSpec(memory_space=pltpu.VMEM)] * 4
         + [pl.BlockSpec(memory_space=pltpu.SMEM)]
-        + [pl.BlockSpec(memory_space=pltpu.VMEM)] * 7,
+        + [pl.BlockSpec(memory_space=pltpu.VMEM)] * 6,
         out_specs=pl.BlockSpec(memory_space=pltpu.VMEM),
         scratch_shapes=[
+            vmem((residual.shape[0], slot_total), jnp.bfloat16),
+            vmem((residual.shape[0], slot_total), jnp.bfloat16),
+            vmem((residual.shape[0], slot_total), jnp.bfloat16),
             vmem(kv_shape, jnp.bfloat16),
             vmem((n_ctx,) + kv_shape, jnp.bfloat16),
             vmem(residual.shape, jnp.bfloat16),
@@ -412,8 +448,8 @@
         ],
         compiler_params=pltpu.CompilerParams(collective_id=collective_id, has_side_effects=True),
         cost_estimate=pl.CostEstimate(flops=flops, bytes_accessed=nbytes, transcendentals=0),
-    )(queries, key_rows, value_rows, residual, block_order, gain, slot_rows, gate_weight, up_weight, down_weight,
-      w_hi, w_lo)
+    )(queries, key_rows, value_rows, residual, block_order, gain, expert_ids, route_weight, gate_weight, up_weight,
+      down_weight)
 
 def kv_gather_kernel(n_ctx, n_exp, group, *refs):
     block, kv_all, s1_send, s1_recv, s2_send, s2_recv = refs
@@ -532,29 +568,6 @@
     ctx_index = lax.axis_index("ctx")
     expert_count = ctx_count * EXP_ROW
     capacity = 2 * shard_rows * TOPK // expert_count
-    flat_ids = expert_ids.reshape(-1)
-    onehot = (flat_ids[:, None] == jnp.arange(expert_count, dtype=jnp.int32)[None, :]).astype(
-        jnp.int32
-    )
-    slot_rank = jnp.sum((jnp.cumsum(onehot, axis=0) - onehot) * onehot, axis=1)
-    slot_index = flat_ids * capacity + slot_rank
-    slot_total = expert_count * capacity
-    slot_rows = jnp.any(
-        slot_index.reshape(shard_rows, TOPK)[None, :, :]
-        == jnp.arange(slot_total, dtype=jnp.int32)[:, None, None],
-        axis=2,
-    ).astype(jnp.bfloat16)
-    slot_weight = jnp.sum(
-        jnp.where(
-            slot_index.reshape(shard_rows, TOPK)[:, :, None]
-            == jnp.arange(slot_total, dtype=jnp.int32)[None, None, :],
-            route_weight[:, :, None],
-            0.0,
-        ),
-        axis=1,
-    )
-    w_hi = slot_weight.astype(jnp.bfloat16)
-    w_lo = (slot_weight - w_hi.astype(jnp.float32)).astype(jnp.bfloat16)
     return moe(
         queries,
         key_rows,
@@ -562,13 +575,12 @@
         residual,
         block_order,
         norm_gain.reshape(1, -1),
-        slot_rows,
+        expert_ids,
+        route_weight,
         (ctx_count, EXP_ROW, capacity, residual.shape[1]),
         gate_weight,
         up_weight,
         down_weight,
-        w_hi,
-        w_lo,
         ctx_count,
         exp_count,
         2,

time: 179 us -> 175 us (0.978)
  other arithmetic: 4.23 us -> 0 us
where the time goes in v11:
time: 175 us
  Pallas kernels  170 us (97%)
  local copies, waits for them, and re-layouts  4.22 us (2%)
    pallas_call x1, Pallas kernels, moe(): pl.pallas_call(functools.partial(moe_kernel, n_ctx, n_exp), out_shape=jax...  170 us
    unnamed x3, local copies, waits for them, and re-layouts  4.22 us

profile of v11, /device:TPU:96, one launch (start us, length us, event | category | flops | bytes accessed | tf_op | source)
XLA Modules:
  0.0 174.6 jit_solution(15868365760581582912)
XLA Ops:
  0.0 1.4 copy.12.refs_6_
  1.4 1.4 copy.13.refs_7_
  2.8 170.4 %shard_map.109 = bf16[64,512]{1,0:T(8,128)(2,1)} custom-call(bf16[64,512]{1,0:T(8,128)(2,1)} %refs_0_.1, bf16[64,256]{1,0:T(8,128)(2,1)} %refs_1_.1, bf16[64,256]{1,0:T(8,128)(2,1)} %refs_2_.1, bf16[64,512]{1,0:T(8,128)(2,1)} %refs_3_.1, s32[32]{0:T(128)} %refs_4_.1, f32[1,512]{1,0:T(1,128)} %bitcast.1, s32[64,8]{1,0:T(8,128)} %copy.12.refs_6_, ...), custom_call_target="tpu_custom_call" | custom-call | flops 2617245696 | bytes 26214400 | tf_op jit(solution)/shard_map/pallas_call | solution.py:408
  173.1 1.5 copy.15

commit v12 on v11

--- a/solution.py
+++ b/solution.py
@@ -133,31 +133,31 @@
             device_id_type=MESH,
         )
 
-    rows_here, topk = expert_ids.shape
-    slot_total = slot_rows.shape[1]
+    topk, rows_here = expert_ids.shape
+    slot_total = slot_rows.shape[0]
     capacity = slot_total // (n_ctx * EXP_ROW)
     ids = expert_ids[...]
-    expert_lane = lax.broadcasted_iota(jnp.int32, (rows_here, n_ctx * EXP_ROW), 1)
-    picks = [(ids[:, i : i + 1] == expert_lane).astype(jnp.float32) for i in range(topk)]
+    expert_sub = lax.broadcasted_iota(jnp.int32, (n_ctx * EXP_ROW, rows_here), 0)
+    picks = [(ids[i : i + 1, :] == expert_sub).astype(jnp.float32) for i in range(topk)]
     per_row = picks[0]
     for i in range(1, topk):
         per_row = per_row + picks[i]
-    earlier = (
-        lax.broadcasted_iota(jnp.int32, (rows_here, rows_here), 1)
-        < lax.broadcasted_iota(jnp.int32, (rows_here, rows_here), 0)
+    later = (
+        lax.broadcasted_iota(jnp.int32, (rows_here, rows_here), 0)
+        < lax.broadcasted_iota(jnp.int32, (rows_here, rows_here), 1)
     ).astype(jnp.bfloat16)
-    before = jnp.dot(earlier, per_row.astype(jnp.bfloat16), preferred_element_type=jnp.float32)
-    slot_lane = lax.broadcasted_iota(jnp.int32, (rows_here, slot_total), 1)
-    chosen = jnp.zeros((rows_here, slot_total), jnp.float32)
-    weight = jnp.zeros((rows_here, slot_total), jnp.float32)
+    before = jnp.dot(per_row.astype(jnp.bfloat16), later, preferred_element_type=jnp.float32)
+    slot_sub = lax.broadcasted_iota(jnp.int32, (slot_total, rows_here), 0)
+    chosen = jnp.zeros((slot_total, rows_here), jnp.float32)
+    weight = jnp.zeros((slot_total, rows_here), jnp.float32)
     weights_in = route_weight[...]
     for i in range(topk):
-        rank = jnp.sum(picks[i] * before, axis=1, keepdims=True)
+        rank = jnp.sum(picks[i] * before, axis=0, keepdims=True)
         before = before + picks[i]
-        slot = ids[:, i : i + 1] * capacity + rank.astype(jnp.int32)
-        hit = slot == slot_lane
+        slot = ids[i : i + 1, :] * capacity + rank.astype(jnp.int32)
+        hit = slot == slot_sub
         chosen = jnp.where(hit, 1.0, chosen)
-        weight = jnp.where(hit, weights_in[:, i : i + 1], weight)
+        weight = jnp.where(hit, weights_in[i : i + 1, :], weight)
     slot_rows[...] = chosen.astype(slot_rows.dtype)
     high = weight.astype(jnp.bfloat16)
     w_hi[...] = high
@@ -229,9 +229,7 @@
     scale = lax.rsqrt(square_sum[:, :1] / D + NORM_EPS)
     mixed_f = mixed[...].astype(jnp.float32)
     normed = (mixed_f * scale * gain[...]).astype(jnp.bfloat16)
-    filled = lax.dot_general(
-        slot_rows[...], normed, (((0,), (0,)), ((), ())), preferred_element_type=jnp.float32
-    )
+    filled = jnp.dot(slot_rows[...], normed, preferred_element_type=jnp.float32)
     outgoing[...] = filled.astype(outgoing.dtype).reshape(outgoing.shape)
 
     def dispatch_copy(p):
@@ -357,9 +355,10 @@
 
     for s in range(n_ctx):
         pltpu.make_async_copy(returned.at[s], returned.at[s], b_recv.at[s]).wait()
-    back = returned[...].reshape(w_hi.shape[1], returned.shape[-1])
-    routed = jnp.dot(w_hi[...], back, preferred_element_type=jnp.float32) + jnp.dot(
-        w_lo[...], back, preferred_element_type=jnp.float32
+    back = returned[...].reshape(w_hi.shape[0], returned.shape[-1])
+    contract = (((0,), (0,)), ((), ()))
+    routed = lax.dot_general(w_hi[...], back, contract, preferred_element_type=jnp.float32) + lax.dot_general(
+        w_lo[...], back, contract, preferred_element_type=jnp.float32
     )
     out[...] = (mixed_f + routed).astype(out.dtype)
 
@@ -413,9 +412,9 @@
         + [pl.BlockSpec(memory_space=pltpu.VMEM)] * 6,
         out_specs=pl.BlockSpec(memory_space=pltpu.VMEM),
         scratch_shapes=[
-            vmem((residual.shape[0], slot_total), jnp.bfloat16),
-            vmem((residual.shape[0], slot_total), jnp.bfloat16),
-            vmem((residual.shape[0], slot_total), jnp.bfloat16),
+            vmem((slot_total, residual.shape[0]), jnp.bfloat16),
+            vmem((slot_total, residual.shape[0]), jnp.bfloat16),
+            vmem((slot_total, residual.shape[0]), jnp.bfloat16),
             vmem(kv_shape, jnp.bfloat16),
             vmem((n_ctx,) + kv_shape, jnp.bfloat16),
             vmem(residual.shape, jnp.bfloat16),
@@ -575,8 +574,8 @@
         residual,
         block_order,
         norm_gain.reshape(1, -1),
-        expert_ids,
-        route_weight,
+        expert_ids.T,
+        route_weight.T,
         (ctx_count, EXP_ROW, capacity, residual.shape[1]),
         gate_weight,
         up_weight,

time: 175 us -> 172 us (0.983)
  local copies, waits for them, and re-layouts: 4.22 us -> 1.47 us
    unnamed x3 -> x1, local copies, waits for them, and re-layouts: 4.22 us -> 1.47 us
where the time goes in v12:
time: 172 us
  Pallas kernels  170 us (99%)
    pallas_call x1, Pallas kernels, moe(): pl.pallas_call(functools.partial(moe_kernel, n_ctx, n_exp), out_shape=jax...  170 us

profile of v12, /device:TPU:96, one launch (start us, length us, event | category | flops | bytes accessed | tf_op | source)
XLA Modules:
  0.0 171.8 jit_solution(16858118694308555657)
XLA Ops:
  0.0 170.3 %shard_map.109 = bf16[64,512]{1,0:T(8,128)(2,1)} custom-call(bf16[64,512]{1,0:T(8,128)(2,1)} %refs_0_.1, bf16[64,256]{1,0:T(8,128)(2,1)} %refs_1_.1, bf16[64,256]{1,0:T(8,128)(2,1)} %refs_2_.1, bf16[64,512]{1,0:T(8,128)(2,1)} %refs_3_.1, s32[32]{0:T(128)} %refs_4_.1, f32[1,512]{1,0:T(1,128)} %bitcast.5, s32[8,64]{1,0:T(8,128)} %bitcast.3, f32[8,64]{1,0:T(8,128)} %bitcast.4, ...), custom_call_target="tpu_custom_call" | custom-call | flops 2617245696 | bytes 26214400 | tf_op jit(solution)/shard_map/pallas_call | solution.py:407
  170.3 1.5 copy.13

commit v13 on v12

--- a/solution.py
+++ b/solution.py
@@ -185,8 +185,19 @@
         key_pos = jnp.where(key_lane // block_rows == b, key_pos + block_order[b] * block_rows, key_pos)
     visible = key_pos <= query_pos
     inv_scale = 1.0 / math.sqrt(HEAD_SIZE)
-    square_part = jnp.zeros((queries.shape[0], 1), jnp.float32)
-    for h in range(queries.shape[1] // HEAD_SIZE):
+    heads = queries.shape[1] // HEAD_SIZE
+
+    def square_copy(r, h):
+        return pltpu.make_async_remote_copy(
+            src_ref=square_block.at[h],
+            dst_ref=square_all.at[me_e, h],
+            send_sem=q_send.at[r, h],
+            recv_sem=q_recv.at[me_e, h],
+            device_id={"exp": r},
+            device_id_type=MESH,
+        )
+
+    for h in range(heads):
         cols = slice(h * HEAD_SIZE, (h + 1) * HEAD_SIZE)
         scores = (
             lax.dot_general(
@@ -205,27 +216,18 @@
         )
         mixed[:, cols] = mixed_h
         mixed_hf = mixed_h.astype(jnp.float32)
-        square_part = square_part + jnp.sum(mixed_hf * mixed_hf, axis=1, keepdims=True)
-    square_block[...] = jnp.broadcast_to(square_part, square_block.shape)
-
-    def square_copy(r):
-        return pltpu.make_async_remote_copy(
-            src_ref=square_block,
-            dst_ref=square_all.at[me_e],
-            send_sem=q_send.at[r],
-            recv_sem=q_recv.at[me_e],
-            device_id={"exp": r},
-            device_id_type=MESH,
-        )
-
-    for k in range(1, n_exp):
-        square_copy(lax.rem(me_e + k, n_exp)).start()
-    pltpu.make_async_copy(square_block, square_all.at[me_e], q_recv.at[me_e]).start()
-    for s in range(n_exp):
-        pltpu.make_async_copy(square_all.at[s], square_all.at[s], q_recv.at[s]).wait()
-    square_sum = square_all[0]
-    for s in range(1, n_exp):
-        square_sum = square_sum + square_all[s]
+        square_h = jnp.sum(mixed_hf * mixed_hf, axis=1, keepdims=True)
+        square_block[h] = jnp.broadcast_to(square_h, square_block.shape[1:])
+        for k in range(1, n_exp):
+            square_copy(lax.rem(me_e + k, n_exp), h).start()
+        pltpu.make_async_copy(square_block.at[h], square_all.at[me_e, h], q_recv.at[me_e, h]).start()
+
+    square_sum = None
+    for h in range(heads):
+        for s in range(n_exp):
+            pltpu.make_async_copy(square_all.at[s, h], square_all.at[s, h], q_recv.at[s, h]).wait()
+            term = square_all[s, h]
+            square_sum = term if square_sum is None else square_sum + term
     scale = lax.rsqrt(square_sum[:, :1] / D + NORM_EPS)
     mixed_f = mixed[...].astype(jnp.float32)
     normed = (mixed_f * scale * gain[...]).astype(jnp.bfloat16)
@@ -367,7 +369,8 @@
         @pl.when(r != me_e)
         def _():
             gather_copy(r).wait_send()
-            square_copy(r).wait_send()
+            for h in range(heads):
+                square_copy(r, h).wait_send()
             for which in range(2):
                 reduce_copy(r, which).wait_send()
 
@@ -397,6 +400,7 @@
     kv_shape = (residual.shape[0], KEY_VALUE_HEADS * HEAD_SIZE)
     mixed = residual
     square_shape = (residual.shape[0], 128)
+    heads = queries.shape[1] // HEAD_SIZE
     hid = gate_weight.shape[-1]
     size = math.prod(out_shape)
     slots = out_shape[0] * out_shape[2] // n_exp
@@ -418,8 +422,8 @@
             vmem(kv_shape, jnp.bfloat16),
             vmem((n_ctx,) + kv_shape, jnp.bfloat16),
             vmem(residual.shape, jnp.bfloat16),
-            vmem(square_shape, jnp.float32),
-            vmem((n_exp,) + square_shape, jnp.float32),
+            vmem((heads,) + square_shape, jnp.float32),
+            vmem((n_exp, heads) + square_shape, jnp.float32),
             vmem(out_shape, jnp.bfloat16),
             vmem(out_shape, jnp.bfloat16),
             vmem(recv_shape, jnp.bfloat16),
@@ -434,8 +438,8 @@
             pltpu.SemaphoreType.DMA((n_ctx,)),
             pltpu.SemaphoreType.DMA((n_exp, 2)),
             pltpu.SemaphoreType.DMA((n_exp, 2)),
-            pltpu.SemaphoreType.DMA((n_exp,)),
-            pltpu.SemaphoreType.DMA((n_exp,)),
+            pltpu.SemaphoreType.DMA((n_exp, heads)),
+            pltpu.SemaphoreType.DMA((n_exp, heads)),
             pltpu.SemaphoreType.DMA((n_ctx,)),
             pltpu.SemaphoreType.DMA((n_ctx,)),
             pltpu.SemaphoreType.DMA((n_exp, 2)),

time: 172 us -> 177 us (1.029)
  the two profiles are of different devices: /device:TPU:96 before, /device:TPU:20 now
where the time goes in v13:
time: 177 us
  Pallas kernels  176 us (99%)
    pallas_call x1, Pallas kernels, moe(): pl.pallas_call(functools.partial(moe_kernel, n_ctx, n_exp), out_shape=jax...  176 us

profile of v13, /device:TPU:20, one launch (start us, length us, event | category | flops | bytes accessed | tf_op | source)
XLA Modules:
  0.0 177.1 jit_solution(92572443904957994)
XLA Ops:
  0.0 175.6 %shard_map.109 = bf16[64,512]{1,0:T(8,128)(2,1)} custom-call(bf16[64,512]{1,0:T(8,128)(2,1)} %refs_0_.1, bf16[64,256]{1,0:T(8,128)(2,1)} %refs_1_.1, bf16[64,256]{1,0:T(8,128)(2,1)} %refs_2_.1, bf16[64,512]{1,0:T(8,128)(2,1)} %refs_3_.1, s32[32]{0:T(128)} %refs_4_.1, f32[1,512]{1,0:T(1,128)} %bitcast.5, s32[8,64]{1,0:T(8,128)} %bitcast.3, f32[8,64]{1,0:T(8,128)} %bitcast.4, ...), custom_call_target="tpu_custom_call" | custom-call | flops 2617245696 | bytes 26214400 | tf_op jit(solution)/shard_map/pallas_call | solution.py:411
  175.6 1.5 copy.13

commit v14 on v12

--- a/solution.py
+++ b/solution.py
@@ -255,20 +255,19 @@
             def _():
                 pltpu.make_async_copy(outgoing.at[p], incoming.at[p], d_recv.at[p]).start()
 
-    parts = ((gate_w, gate_stage, gate_recv), (up_w, up_stage, up_recv))
-
-    def reduce_copy(j, which):
-        _, stage, recv = parts[which]
+    stage, recv = gate_stage, gate_recv
+
+    def reduce_copy(j):
         return pltpu.make_async_remote_copy(
             src_ref=stage.at[j],
             dst_ref=recv.at[me_e],
-            send_sem=r_send.at[j, which],
-            recv_sem=r_recv.at[me_e, which],
+            send_sem=r_send.at[j],
+            recv_sem=r_recv.at[me_e],
             device_id={"exp": j},
             device_id_type=MESH,
         )
 
-    rows = gate_stage.shape[2]
+    rows = stage.shape[3]
     for t in range(n_exp):
         j = lax.rem(plane + me_e + t, n_exp)
         for y in range(per_chunk):
@@ -277,29 +276,26 @@
         first = pl.multiple_of(j * per_chunk, per_chunk)
         for k in range(EXP_ROW):
             x = incoming[pl.ds(first, per_chunk), k].reshape(rows, incoming.shape[-1])
-            for w, stage, _ in parts:
-                stage[j, k] = jnp.dot(x, w[k], preferred_element_type=jnp.float32).astype(
+            for which, w in enumerate((gate_w, up_w)):
+                stage[j, which, k] = jnp.dot(x, w[k], preferred_element_type=jnp.float32).astype(
                     stage.dtype
                 )
 
         @pl.when(j != me_e)
         def _():
-            for which in range(2):
-                reduce_copy(j, which).start()
+            reduce_copy(j).start()
 
         @pl.when(j == me_e)
         def _():
-            for which, (_, stage, recv) in enumerate(parts):
-                pltpu.make_async_copy(stage.at[j], recv.at[j], r_recv.at[j, which]).start()
+            pltpu.make_async_copy(stage.at[j], recv.at[j], r_recv.at[j]).start()
 
     for s in range(n_exp):
-        for which, (_, _, recv) in enumerate(parts):
-            pltpu.make_async_copy(recv.at[s], recv.at[s], r_recv.at[s, which]).wait()
-    gate_sum = gate_recv[0].astype(jnp.float32)
-    up_sum = up_recv[0].astype(jnp.float32)
+        pltpu.make_async_copy(recv.at[s], recv.at[s], r_recv.at[s]).wait()
+    gate_sum = recv[0, 0].astype(jnp.float32)
+    up_sum = recv[0, 1].astype(jnp.float32)
     for s in range(1, n_exp):
-        gate_sum = gate_sum + gate_recv[s].astype(jnp.float32)
-        up_sum = up_sum + up_recv[s].astype(jnp.float32)
+        gate_sum = gate_sum + recv[s, 0].astype(jnp.float32)
+        up_sum = up_sum + recv[s, 1].astype(jnp.float32)
     hidden_mine[...] = (gate_sum / (1.0 + jnp.exp(-gate_sum)) * up_sum).astype(hidden_mine.dtype)
 
     def gather_copy(r):
@@ -368,8 +364,7 @@
         def _():
             gather_copy(r).wait_send()
             square_copy(r).wait_send()
-            for which in range(2):
-                reduce_copy(r, which).wait_send()
+            reduce_copy(r).wait_send()
 
     for p in range(n_ctx):
 
@@ -422,10 +417,10 @@
             vmem((n_exp,) + square_shape, jnp.float32),
             vmem(out_shape, jnp.bfloat16),
             vmem(out_shape, jnp.bfloat16),
-            vmem(recv_shape, jnp.bfloat16),
-            vmem(recv_shape, jnp.bfloat16),
-            vmem(recv_shape, jnp.bfloat16),
-            vmem(recv_shape, jnp.bfloat16),
+            vmem((n_exp, 2) + recv_shape[1:], jnp.bfloat16),
+            vmem((8, 128), jnp.bfloat16),
+            vmem((n_exp, 2) + recv_shape[1:], jnp.bfloat16),
+            vmem((8, 128), jnp.bfloat16),
             vmem(recv_shape[1:], jnp.bfloat16),
             vmem(recv_shape, jnp.bfloat16),
             vmem(out_shape, jnp.bfloat16),
@@ -438,8 +433,8 @@
             pltpu.SemaphoreType.DMA((n_exp,)),
             pltpu.SemaphoreType.DMA((n_ctx,)),
             pltpu.SemaphoreType.DMA((n_ctx,)),
-            pltpu.SemaphoreType.DMA((n_exp, 2)),
-            pltpu.SemaphoreType.DMA((n_exp, 2)),
+            pltpu.SemaphoreType.DMA((n_exp,)),
+            pltpu.SemaphoreType.DMA((n_exp,)),
             pltpu.SemaphoreType.DMA((n_exp,)),
             pltpu.SemaphoreType.DMA((n_exp,)),
             pltpu.SemaphoreType.DMA((n_ctx,)),

time: 172 us -> 171 us (level)
  no operation moved by 1% of the time
where the time goes in v14:
time: 171 us
  Pallas kernels  170 us (99%)
    pallas_call x1, Pallas kernels, moe(): pl.pallas_call(functools.partial(moe_kernel, n_ctx, n_exp), out_shape=jax...  170 us

profile of v14, /device:TPU:96, one launch (start us, length us, event | category | flops | bytes accessed | tf_op | source)
XLA Modules:
  0.0 171.2 jit_solution(12660551442877608024)
XLA Ops:
  0.0 169.7 %shard_map.109 = bf16[64,512]{1,0:T(8,128)(2,1)} custom-call(bf16[64,512]{1,0:T(8,128)(2,1)} %refs_0_.1, bf16[64,256]{1,0:T(8,128)(2,1)} %refs_1_.1, bf16[64,256]{1,0:T(8,128)(2,1)} %refs_2_.1, bf16[64,512]{1,0:T(8,128)(2,1)} %refs_3_.1, s32[32]{0:T(128)} %refs_4_.1, f32[1,512]{1,0:T(1,128)} %bitcast.5, s32[8,64]{1,0:T(8,128)} %bitcast.3, f32[8,64]{1,0:T(8,128)} %bitcast.4, ...), custom_call_target="tpu_custom_call" | custom-call | flops 2617245696 | bytes 26214400 | tf_op jit(solution)/shard_map/pallas_call | solution.py:402
  169.7 1.5 copy.13

commit v15 on v14

--- a/solution.py
+++ b/solution.py
@@ -206,7 +206,11 @@
         mixed[:, cols] = mixed_h
         mixed_hf = mixed_h.astype(jnp.float32)
         square_part = square_part + jnp.sum(mixed_hf * mixed_hf, axis=1, keepdims=True)
-    square_block[...] = jnp.broadcast_to(square_part, square_block.shape)
+    rows_q = queries.shape[0]
+    padded = jnp.concatenate(
+        [jnp.broadcast_to(square_part, (rows_q, 128)), jnp.zeros((128 - rows_q, 128), jnp.float32)], axis=0
+    )
+    square_block[...] = jnp.transpose(padded)[: square_block.shape[0], :]
 
     def square_copy(r):
         return pltpu.make_async_remote_copy(
@@ -226,7 +230,10 @@
     square_sum = square_all[0]
     for s in range(1, n_exp):
         square_sum = square_sum + square_all[s]
-    scale = lax.rsqrt(square_sum[:, :1] / D + NORM_EPS)
+    back_rows = jnp.concatenate(
+        [square_sum, jnp.zeros((128 - square_sum.shape[0], 128), jnp.float32)], axis=0
+    )
+    scale = lax.rsqrt(jnp.transpose(back_rows)[: queries.shape[0], :1] / D + NORM_EPS)
     mixed_f = mixed[...].astype(jnp.float32)
     normed = (mixed_f * scale * gain[...]).astype(jnp.bfloat16)
     filled = jnp.dot(slot_rows[...], normed, preferred_element_type=jnp.float32)
@@ -391,7 +398,7 @@
     slot_total = out_shape[0] * out_shape[1] * out_shape[2]
     kv_shape = (residual.shape[0], KEY_VALUE_HEADS * HEAD_SIZE)
     mixed = residual
-    square_shape = (residual.shape[0], 128)
+    square_shape = (8, 128)
     hid = gate_weight.shape[-1]
     size = math.prod(out_shape)
     slots = out_shape[0] * out_shape[2] // n_exp

time: 171 us -> 170 us (level)
  Pallas kernels: 170 us -> 168 us
where the time goes in v15:
time: 170 us
  Pallas kernels  168 us (99%)
    pallas_call x1, Pallas kernels, moe(): pl.pallas_call(functools.partial(moe_kernel, n_ctx, n_exp), out_shape=jax...  168 us

profile of v15, /device:TPU:96, one launch (start us, length us, event | category | flops | bytes accessed | tf_op | source)
XLA Modules:
  0.0 169.7 jit_solution(2222288425131530704)
XLA Ops:
  0.0 168.2 %shard_map.109 = bf16[64,512]{1,0:T(8,128)(2,1)} custom-call(bf16[64,512]{1,0:T(8,128)(2,1)} %refs_0_.1, bf16[64,256]{1,0:T(8,128)(2,1)} %refs_1_.1, bf16[64,256]{1,0:T(8,128)(2,1)} %refs_2_.1, bf16[64,512]{1,0:T(8,128)(2,1)} %refs_3_.1, s32[32]{0:T(128)} %refs_4_.1, f32[1,512]{1,0:T(1,128)} %bitcast.5, s32[8,64]{1,0:T(8,128)} %bitcast.3, f32[8,64]{1,0:T(8,128)} %bitcast.4, ...), custom_call_target="tpu_custom_call" | custom-call | flops 2617245696 | bytes 26214400 | tf_op jit(solution)/shard_map/pallas_call | solution.py:409
  168.2 1.5 copy.13

commit v16 on v15

--- a/solution.py
+++ b/solution.py
@@ -163,20 +163,7 @@
     w_hi[...] = high
     w_lo[...] = (weight - high.astype(jnp.float32)).astype(jnp.bfloat16)
 
-    for h in range(halves):
-        z_s = lax.rem(plane + q + h * (planes // halves), planes)
-        for y in range(per_chunk):
-            s = z_s * per_chunk + y
-            pltpu.make_async_copy(kv_all.at[s], kv_all.at[s], s1_recv.at[s]).wait()
-        for r in range(1, group):
-            second_copy(h, r).start()
-    for h in range(halves):
-        for r in range(1, group):
-            second_copy(h, r).wait_recv()
-
     total_rows = kv_all.shape[0] * kv_all.shape[1]
-    keys = kv_all[:, :, :HEAD_SIZE].reshape(total_rows, HEAD_SIZE)
-    values = kv_all[:, :, HEAD_SIZE:].reshape(total_rows, HEAD_SIZE)
     block_rows = kv_all.shape[1]
     query_pos = block_order[me_c] * block_rows + lax.broadcasted_iota(jnp.int32, (queries.shape[0], 1), 0)
     key_lane = lax.broadcasted_iota(jnp.int32, (1, total_rows), 1)
@@ -184,6 +171,21 @@
     for b in range(kv_all.shape[0]):
         key_pos = jnp.where(key_lane // block_rows == b, key_pos + block_order[b] * block_rows, key_pos)
     visible = key_pos <= query_pos
+
+    for h in range(halves):
+        z_s = lax.rem(plane + q + h * (planes // halves), planes)
+        for y in range(per_chunk):
+            s = z_s * per_chunk + y
+            pltpu.make_async_copy(kv_all.at[s], kv_all.at[s], s1_recv.at[s]).wait()
+        for r in range(1, group):
+            second_copy(h, r).start()
+    for h in range(halves):
+        for r in range(1, group):
+            second_copy(h, r).wait_recv()
+
+    total_rows = kv_all.shape[0] * kv_all.shape[1]
+    keys = kv_all[:, :, :HEAD_SIZE].reshape(total_rows, HEAD_SIZE)
+    values = kv_all[:, :, HEAD_SIZE:].reshape(total_rows, HEAD_SIZE)
     inv_scale = 1.0 / math.sqrt(HEAD_SIZE)
     square_part = jnp.zeros((queries.shape[0], 1), jnp.float32)
     for h in range(queries.shape[1] // HEAD_SIZE):

time: 170 us -> 171 us (level)
  the two profiles are of different devices: /device:TPU:96 before, /device:TPU:4 now
where the time goes in v16:
time: 171 us
  Pallas kernels  169 us (99%)
    pallas_call x1, Pallas kernels, moe(): pl.pallas_call(functools.partial(moe_kernel, n_ctx, n_exp), out_shape=jax...  169 us

profile of v16, /device:TPU:4, one launch (start us, length us, event | category | flops | bytes accessed | tf_op | source)
XLA Modules:
  0.0 170.6 jit_solution(4517980661815029270)
XLA Ops:
  0.0 169.1 %shard_map.109 = bf16[64,512]{1,0:T(8,128)(2,1)} custom-call(bf16[64,512]{1,0:T(8,128)(2,1)} %refs_0_.1, bf16[64,256]{1,0:T(8,128)(2,1)} %refs_1_.1, bf16[64,256]{1,0:T(8,128)(2,1)} %refs_2_.1, bf16[64,512]{1,0:T(8,128)(2,1)} %refs_3_.1, s32[32]{0:T(128)} %refs_4_.1, f32[1,512]{1,0:T(1,128)} %bitcast.5, s32[8,64]{1,0:T(8,128)} %bitcast.3, f32[8,64]{1,0:T(8,128)} %bitcast.4, ...), custom_call_target="tpu_custom_call" | custom-call | flops 2617245696 | bytes 26214400 | tf_op jit(solution)/shard_map/pallas_call | solution.py:411
  169.1 1.5 copy.13

commit v17 on v15

--- a/solution.py
+++ b/solution.py
@@ -159,9 +159,10 @@
         chosen = jnp.where(hit, 1.0, chosen)
         weight = jnp.where(hit, weights_in[i : i + 1, :], weight)
     slot_rows[...] = chosen.astype(slot_rows.dtype)
-    high = weight.astype(jnp.bfloat16)
+    weight_t = jnp.transpose(weight)
+    high = weight_t.astype(jnp.bfloat16)
     w_hi[...] = high
-    w_lo[...] = (weight - high.astype(jnp.float32)).astype(jnp.bfloat16)
+    w_lo[...] = (weight_t - high.astype(jnp.float32)).astype(jnp.bfloat16)
 
     for h in range(halves):
         z_s = lax.rem(plane + q + h * (planes // halves), planes)
@@ -358,10 +359,9 @@
 
     for s in range(n_ctx):
         pltpu.make_async_copy(returned.at[s], returned.at[s], b_recv.at[s]).wait()
-    back = returned[...].reshape(w_hi.shape[0], returned.shape[-1])
-    contract = (((0,), (0,)), ((), ()))
-    routed = lax.dot_general(w_hi[...], back, contract, preferred_element_type=jnp.float32) + lax.dot_general(
-        w_lo[...], back, contract, preferred_element_type=jnp.float32
+    back = returned[...].reshape(w_hi.shape[1], returned.shape[-1])
+    routed = jnp.dot(w_hi[...], back, preferred_element_type=jnp.float32) + jnp.dot(
+        w_lo[...], back, preferred_element_type=jnp.float32
     )
     out[...] = (mixed_f + routed).astype(out.dtype)
 
@@ -415,8 +415,8 @@
         out_specs=pl.BlockSpec(memory_space=pltpu.VMEM),
         scratch_shapes=[
             vmem((slot_total, residual.shape[0]), jnp.bfloat16),
-            vmem((slot_total, residual.shape[0]), jnp.bfloat16),
-            vmem((slot_total, residual.shape[0]), jnp.bfloat16),
+            vmem((residual.shape[0], slot_total), jnp.bfloat16),
+            vmem((residual.shape[0], slot_total), jnp.bfloat16),
             vmem(kv_shape, jnp.bfloat16),
             vmem((n_ctx,) + kv_shape, jnp.bfloat16),
             vmem(residual.shape, jnp.bfloat16),

time: 170 us -> 171 us (level)
  the two profiles are of different devices: /device:TPU:96 before, /device:TPU:4 now
where the time goes in v17:
time: 171 us; the launch traced here: 170 us
  Pallas kernels  169 us (99%)
    pallas_call x1, Pallas kernels, moe(): pl.pallas_call(functools.partial(moe_kernel, n_ctx, n_exp), out_shape=jax...  169 us

profile of v17, /device:TPU:4, one launch (start us, length us, event | category | flops | bytes accessed | tf_op | source)
XLA Modules:
  0.0 170.5 jit_solution(12645435607090737083)
XLA Ops:
  0.0 169.0 %shard_map.109 = bf16[64,512]{1,0:T(8,128)(2,1)} custom-call(bf16[64,512]{1,0:T(8,128)(2,1)} %refs_0_.1, bf16[64,256]{1,0:T(8,128)(2,1)} %refs_1_.1, bf16[64,256]{1,0:T(8,128)(2,1)} %refs_2_.1, bf16[64,512]{1,0:T(8,128)(2,1)} %refs_3_.1, s32[32]{0:T(128)} %refs_4_.1, f32[1,512]{1,0:T(1,128)} %bitcast.5, s32[8,64]{1,0:T(8,128)} %bitcast.3, f32[8,64]{1,0:T(8,128)} %bitcast.4, ...), custom_call_target="tpu_custom_call" | custom-call | flops 2617245696 | bytes 26214400 | tf_op jit(solution)/shard_map/pallas_call | solution.py:409
  169.0 1.5 copy.13
